TPU v7x, 32 devices: a whole 2x2x4 slice. The times are simulated.
32 devices in a mesh: users: 16 (over z, y, x), rep: 2 (over core).
Axes of the slice: x: 2, y: 2, z: 4, core: 2. Of those that a mesh axis runs over, the one named last changes fastest.
Arguments:
- user_factors: float32 [16384, 256], P('users'), may hold values from -1.5 to 1.5
- user_accum: float32 [16384, 256], P('users'), may hold values from 0.5 to 8
- item_factors: float32 [4096, 256], P('users'), may hold values from -1.5 to 1.5
- item_accum: float32 [4096, 256], P('users'), may hold values from 0.5 to 8
- tile_counts: bfloat16 [16, 2, 128, 128, 128], P('users', 'rep'), may hold values from 0 to 20, as said below
- tile_user: int32 [16, 2, 128], P('users', 'rep'), may hold values from 0 to 7
- tile_item: int32 [16, 2, 128], P('users', 'rep'), may hold values from 0 to 31, as said below
- send_list: int32 [16, 2, 16], P('users', 'rep'), may hold values from 0 to 2, as said below
Outputs:
- new_users: float32 [16384, 256], P('users')
- new_user_accum: float32 [16384, 256], P('users')
- new_items: float32 [4096, 256], P('users')
- new_item_accum: float32 [4096, 256], P('users')
Inputs may be any that keep to these rules, and one draw needn't show every extreme that they name: `tile_counts`: zero means no interaction. `tile_item`: panel b belongs to owner b // 2. Device (q, r) uses at most one panel of each owner o, namely o * 2 + send_list[o, r, q], and only where send_list[o, r, q] < 2. `send_list`: the value 2 means that requester q uses no panel of owner o.
All inputs are finite; a program needn't handle non-finite values.
Results may differ from a plain program's by a relative error of at most 0.0026.
Values may be sent and summed in bfloat16 or wider, within the bound.
No kernel may reach another device: no remote copies, remote signals or barrier semaphores. Data moves between devices by JAX's collectives and lax.ppermute only.
A program may use at most 128 MiB of HBM per device.

v0:
```python
import math

import jax
import jax.numpy as jnp
from jax import lax
from jax.sharding import PartitionSpec as P

CONF_SLOPE = 0.5
ERR_SCALE = 1.0 / 64.0


def tile_terms(user_strip, panels, counts, users_idx, fetch_index, slot_index, slot_count):
    tile_count = counts.shape[0]
    group_size = math.gcd(tile_count, 32)
    group_count = tile_count // group_size
    side = counts.shape[-1]
    width = panels.shape[-1]

    def tile_step(totals, inputs):
        user_total, slot_total = totals
        block_counts, block_user, block_fetch, block_slot = inputs
        user_rows = user_strip[block_user]
        item_rows = panels[block_fetch]
        predicted = jnp.einsum(
            "gur,gir->gui", user_rows, item_rows, preferred_element_type=jnp.float32
        )
        amount = block_counts.astype(jnp.float32)
        confidence = 1.0 + CONF_SLOPE * amount
        preference = jnp.where(amount > 0, 1.0, 0.0).astype(jnp.float32)
        weighted_err = (confidence * (predicted - preference) * ERR_SCALE).astype(jnp.bfloat16)
        user_part = jnp.einsum(
            "gui,gir->gur", weighted_err, item_rows, preferred_element_type=jnp.float32
        )
        item_part = jnp.einsum(
            "gui,gur->gir", weighted_err, user_rows, preferred_element_type=jnp.float32
        )
        user_total = user_total.at[block_user].add(user_part)
        slot_total = slot_total.at[block_slot].add(item_part)
        return ((user_total, slot_total), None)

    start = (
        jnp.zeros((user_strip.shape[0], side, width), jnp.float32),
        jnp.zeros((slot_count, side, width), jnp.float32),
    )
    inputs = (
        counts.reshape(group_count, group_size, side, side),
        users_idx.reshape(group_count, group_size),
        fetch_index.reshape(group_count, group_size),
        slot_index.reshape(group_count, group_size),
    )
    (user_total, slot_total), _ = lax.scan(tile_step, start, inputs)
    return (user_total, slot_total)


def adagrad(factors, accum, grad):
    new_accum = accum + grad * grad
    return (factors - grad / jnp.sqrt(new_accum), new_accum)


def local(
    user_factors, user_accum, item_factors, item_accum, tile_counts, tile_user, tile_item, send_list
):
    tile_size = tile_counts.shape[-1]
    feat_width = user_factors.shape[1]
    user_strip = user_factors.astype(jnp.bfloat16).reshape(-1, tile_size, feat_width)
    owned_panels = item_factors.astype(jnp.bfloat16).reshape(-1, tile_size, feat_width)
    panels_own = owned_panels.shape[0]
    peer_count = lax.axis_size("users")
    counts = tile_counts[0, 0]
    users_idx = tile_user[0, 0]
    items_idx = tile_item[0, 0]
    send_row = send_list[0, 0]
    slot_index = items_idx // panels_own
    outgoing = owned_panels[jnp.minimum(send_row, panels_own - 1)]
    panels = lax.all_to_all(outgoing, "users", split_axis=0, concat_axis=0, tiled=True)
    user_part, slot_part = tile_terms(
        user_strip, panels, counts, users_idx, slot_index, slot_index, peer_count
    )
    returned = lax.all_to_all(
        slot_part.astype(jnp.bfloat16), "users", split_axis=0, concat_axis=0, tiled=True
    )
    selector = (send_row[None, :] == jnp.arange(panels_own, dtype=jnp.int32)[:, None]).astype(
        jnp.bfloat16
    )
    item_part = jnp.einsum("kq,qir->kir", selector, returned, preferred_element_type=jnp.float32)
    item_part = item_part.reshape(-1, feat_width)
    user_grad = lax.psum(user_part.reshape(-1, feat_width), "rep")
    new_users, new_user_accum = adagrad(user_factors, user_accum, user_grad)
    item_grad = lax.psum(item_part, "rep")
    new_items, new_item_accum = adagrad(item_factors, item_accum, item_grad)
    return (new_users, new_user_accum, new_items, new_item_accum)


def solution(mesh):
    return jax.shard_map(
        local,
        mesh=mesh,
        in_specs=(
            P("users", None),
            P("users", None),
            P("users", None),
            P("users", None),
            P("users", "rep", None, None, None),
            P("users", "rep", None),
            P("users", "rep", None),
            P("users", "rep", None),
        ),
        out_specs=(P("users", None), P("users", None), P("users", None), P("users", None)),
        check_vma=False,
    )
```

profile of v0, /device:TPU:0, one launch (start us, length us, event | category | flops | bytes accessed | tf_op | source)
XLA Modules:
  0.0 230.2 jit_solution(15211641022157744401)
XLA Ops:
  10.4 8.3 %all-to-all-start = ((bf16[16,128,256]{2,1,0:T(8,128)(2,1)}), bf16[16,128,256]{2,1,0:T(8,128)(2,1)S(1)}, u32[]{:S(2)}, u32[]{:S(2)}) async-start(bf16[16,128,256]{2,1,0:T(8,128)(2,1)} %gather_fusion.2), calls=%async_computation | async-start | bytes 2097152 | tf_op jit(solution)/shard_map/all_to_all | solution.py:75
  21.7 21.4 %all-to-all-done = bf16[16,128,256]{2,1,0:T(8,128)(2,1)S(1)} async-done(((bf16[16,128,256]{2,1,0:T(8,128)(2,1)}), bf16[16,128,256]{2,1,0:T(8,128)(2,1)S(1)}, u32[]{:S(2)}, u32[]{:S(2)}) %all-to-all-start) | async-done | bytes 1048608 | tf_op jit(solution)/shard_map/all_to_all | solution.py:75
  44.4 123.7 %while.13 = (s32[]{:T(128)}, f32[8,128,256]{2,1,0:T(8,128)S(1)}, f32[16,128,256]{2,1,0:T(8,128)S(1)}, s32[4,32]{1,0:T(4,128)S(1)}, bf16[4,32,128,128]{3,2,1,0:T(...) while((s32[]{:T(128)}, f32[8,128,256]{2,1,0:T(8,128)S(1)}, ...), condition=%wide.region_3.4_spmd, body=%wide.region_0.3_spmd.sunk | while | flops 812124352 | bytes 67118496 | solution.py:51
  44.5 3.2 %gather_fusion.1 = bf16[32,128,256]{2,1,0:T(8,128)(2,1)} fusion(bf16[16,128,256]{2,1,0:T(8,128)(2,1)} %get-tuple-element.173, s32[1024]{0:T(1024)S(1)} %pad_clamp_fusion.6), kind=kCustom, calls=%fused_computation.1.clone.1 | custom fusion | bytes 4194432 | tf_op jit(solution)/shard_map/while/body/eval_jaxpr/gather | solution.py:23
  50.8 3.4 %fusion.43 = bf16[32,128,128]{2,1,0:T(8,128)(2,1)S(1)} fusion(bf16[32,128,256]{2,1,0:T(8,128)(2,1)} %gather_fusion, bf16[32,128,256]{2,1,0:T(8,128)(2,1)} %gather_fusion.1, bf16[4,32,128,128]{3,2,1,0:T(8,128)(2,1)} %get-tuple-element.170, s32[]{:T(128)S(6)} %copy.28), kind=kOutput, calls=%fused_computation.11.clone.1 | convolution fusion | flops 273154048 | bytes 6291460 | tf_op jit(solution)/shard_map/while/body/eval_jaxpr/gur,gir->gui/dot_general | solution.py:24
  57.9 6.5 %scatter_fusion.1 = f32[16,128,256]{2,1,0:T(8,128)S(1)} fusion(f32[16,128,256]{2,1,0:T(8,128)S(1)} %get-tuple-element.159, s32[32]{0:T(128)S(1)} %get-tuple-element.147, f32[32,128,256]{2,1,0:T(8,128)} %fusion.45), kind=kCustom, calls=%fused_computation.4.clone.1 | custom fusion | flops 1048576 | bytes 12583040 | tf_op jit(solution)/shard_map/while/body/eval_jaxpr/scatter-add | solution.py:38
  64.3 4.5 %fusion.44 = f32[32,128,256]{2,1,0:T(8,128)} fusion(bf16[32,128,128]{2,1,0:T(8,128)(2,1)} %copy-done.3, bf16[32,128,256]{2,1,0:T(8,128)(2,1)} %gather_fusion.1), kind=kOutput, calls=%fused_computation.43.clone.1 | convolution fusion | flops 268435456 | bytes 7340032 | tf_op jit(solution)/shard_map/while/body/eval_jaxpr/gui,gir->gur/dot_general | solution.py:31
  68.9 6.4 %scatter_fusion = f32[8,128,256]{2,1,0:T(8,128)S(1)} fusion(f32[8,128,256]{2,1,0:T(8,128)S(1)} %get-tuple-element.158, s32[32]{0:T(128)S(1)} %get-tuple-element.146, f32[32,128,256]{2,1,0:T(8,128)} %fusion.44), kind=kCustom, calls=%fused_computation.3.clone.1 | custom fusion | flops 1048576 | bytes 12583040 | tf_op jit(solution)/shard_map/while/body/eval_jaxpr/scatter-add | solution.py:37
  75.4 3.2 %gather_fusion.1 = bf16[32,128,256]{2,1,0:T(8,128)(2,1)} fusion(bf16[16,128,256]{2,1,0:T(8,128)(2,1)} %get-tuple-element.173, s32[1024]{0:T(1024)S(1)} %pad_clamp_fusion.6), kind=kCustom, calls=%fused_computation.1.clone.1 | custom fusion | bytes 4194432 | tf_op jit(solution)/shard_map/while/body/eval_jaxpr/gather | solution.py:23
  81.7 3.4 %fusion.43 = bf16[32,128,128]{2,1,0:T(8,128)(2,1)S(1)} fusion(bf16[32,128,256]{2,1,0:T(8,128)(2,1)} %gather_fusion, bf16[32,128,256]{2,1,0:T(8,128)(2,1)} %gather_fusion.1, bf16[4,32,128,128]{3,2,1,0:T(8,128)(2,1)} %get-tuple-element.170, s32[]{:T(128)S(6)} %copy.28), kind=kOutput, calls=%fused_computation.11.clone.1 | convolution fusion | flops 273154048 | bytes 6291460 | tf_op jit(solution)/shard_map/while/body/eval_jaxpr/gur,gir->gui/dot_general | solution.py:24
  88.8 6.5 %scatter_fusion.1 = f32[16,128,256]{2,1,0:T(8,128)S(1)} fusion(f32[16,128,256]{2,1,0:T(8,128)S(1)} %get-tuple-element.159, s32[32]{0:T(128)S(1)} %get-tuple-element.147, f32[32,128,256]{2,1,0:T(8,128)} %fusion.45), kind=kCustom, calls=%fused_computation.4.clone.1 | custom fusion | flops 1048576 | bytes 12583040 | tf_op jit(solution)/shard_map/while/body/eval_jaxpr/scatter-add | solution.py:38
  95.3 4.6 %fusion.44 = f32[32,128,256]{2,1,0:T(8,128)} fusion(bf16[32,128,128]{2,1,0:T(8,128)(2,1)} %copy-done.3, bf16[32,128,256]{2,1,0:T(8,128)(2,1)} %gather_fusion.1), kind=kOutput, calls=%fused_computation.43.clone.1 | convolution fusion | flops 268435456 | bytes 7340032 | tf_op jit(solution)/shard_map/while/body/eval_jaxpr/gui,gir->gur/dot_general | solution.py:31
  99.8 6.4 %scatter_fusion = f32[8,128,256]{2,1,0:T(8,128)S(1)} fusion(f32[8,128,256]{2,1,0:T(8,128)S(1)} %get-tuple-element.158, s32[32]{0:T(128)S(1)} %get-tuple-element.146, f32[32,128,256]{2,1,0:T(8,128)} %fusion.44), kind=kCustom, calls=%fused_computation.3.clone.1 | custom fusion | flops 1048576 | bytes 12583040 | tf_op jit(solution)/shard_map/while/body/eval_jaxpr/scatter-add | solution.py:37
  112.6 3.4 %fusion.43 = bf16[32,128,128]{2,1,0:T(8,128)(2,1)S(1)} fusion(bf16[32,128,256]{2,1,0:T(8,128)(2,1)} %gather_fusion, bf16[32,128,256]{2,1,0:T(8,128)(2,1)} %gather_fusion.1, bf16[4,32,128,128]{3,2,1,0:T(8,128)(2,1)} %get-tuple-element.170, s32[]{:T(128)S(6)} %copy.28), kind=kOutput, calls=%fused_computation.11.clone.1 | convolution fusion | flops 273154048 | bytes 6291460 | tf_op jit(solution)/shard_map/while/body/eval_jaxpr/gur,gir->gui/dot_general | solution.py:24
  119.7 6.5 %scatter_fusion.1 = f32[16,128,256]{2,1,0:T(8,128)S(1)} fusion(f32[16,128,256]{2,1,0:T(8,128)S(1)} %get-tuple-element.159, s32[32]{0:T(128)S(1)} %get-tuple-element.147, f32[32,128,256]{2,1,0:T(8,128)} %fusion.45), kind=kCustom, calls=%fused_computation.4.clone.1 | custom fusion | flops 1048576 | bytes 12583040 | tf_op jit(solution)/shard_map/while/body/eval_jaxpr/scatter-add | solution.py:38
  126.2 4.6 %fusion.44 = f32[32,128,256]{2,1,0:T(8,128)} fusion(bf16[32,128,128]{2,1,0:T(8,128)(2,1)} %copy-done.3, bf16[32,128,256]{2,1,0:T(8,128)(2,1)} %gather_fusion.1), kind=kOutput, calls=%fused_computation.43.clone.1 | convolution fusion | flops 268435456 | bytes 7340032 | tf_op jit(solution)/shard_map/while/body/eval_jaxpr/gui,gir->gur/dot_general | solution.py:31
  130.7 6.5 %scatter_fusion = f32[8,128,256]{2,1,0:T(8,128)S(1)} fusion(f32[8,128,256]{2,1,0:T(8,128)S(1)} %get-tuple-element.158, s32[32]{0:T(128)S(1)} %get-tuple-element.146, f32[32,128,256]{2,1,0:T(8,128)} %fusion.44), kind=kCustom, calls=%fused_computation.3.clone.1 | custom fusion | flops 1048576 | bytes 12583040 | tf_op jit(solution)/shard_map/while/body/eval_jaxpr/scatter-add | solution.py:37
  137.3 3.2 %gather_fusion.1 = bf16[32,128,256]{2,1,0:T(8,128)(2,1)} fusion(bf16[16,128,256]{2,1,0:T(8,128)(2,1)} %get-tuple-element.173, s32[1024]{0:T(1024)S(1)} %pad_clamp_fusion.6), kind=kCustom, calls=%fused_computation.1.clone.1 | custom fusion | bytes 4194432 | tf_op jit(solution)/shard_map/while/body/eval_jaxpr/gather | solution.py:23
  143.6 3.4 %fusion.43 = bf16[32,128,128]{2,1,0:T(8,128)(2,1)S(1)} fusion(bf16[32,128,256]{2,1,0:T(8,128)(2,1)} %gather_fusion, bf16[32,128,256]{2,1,0:T(8,128)(2,1)} %gather_fusion.1, bf16[4,32,128,128]{3,2,1,0:T(8,128)(2,1)} %get-tuple-element.170, s32[]{:T(128)S(6)} %copy.28), kind=kOutput, calls=%fused_computation.11.clone.1 | convolution fusion | flops 273154048 | bytes 6291460 | tf_op jit(solution)/shard_map/while/body/eval_jaxpr/gur,gir->gui/dot_general | solution.py:24
  150.6 6.5 %scatter_fusion.1 = f32[16,128,256]{2,1,0:T(8,128)S(1)} fusion(f32[16,128,256]{2,1,0:T(8,128)S(1)} %get-tuple-element.159, s32[32]{0:T(128)S(1)} %get-tuple-element.147, f32[32,128,256]{2,1,0:T(8,128)} %fusion.45), kind=kCustom, calls=%fused_computation.4.clone.1 | custom fusion | flops 1048576 | bytes 12583040 | tf_op jit(solution)/shard_map/while/body/eval_jaxpr/scatter-add | solution.py:38
  157.1 4.6 %fusion.44 = f32[32,128,256]{2,1,0:T(8,128)} fusion(bf16[32,128,128]{2,1,0:T(8,128)(2,1)} %copy-done.3, bf16[32,128,256]{2,1,0:T(8,128)(2,1)} %gather_fusion.1), kind=kOutput, calls=%fused_computation.43.clone.1 | convolution fusion | flops 268435456 | bytes 7340032 | tf_op jit(solution)/shard_map/while/body/eval_jaxpr/gui,gir->gur/dot_general | solution.py:31
  161.7 6.4 %scatter_fusion = f32[8,128,256]{2,1,0:T(8,128)S(1)} fusion(f32[8,128,256]{2,1,0:T(8,128)S(1)} %get-tuple-element.158, s32[32]{0:T(128)S(1)} %get-tuple-element.146, f32[32,128,256]{2,1,0:T(8,128)} %fusion.44), kind=kCustom, calls=%fused_computation.3.clone.1 | custom fusion | flops 1048576 | bytes 12583040 | tf_op jit(solution)/shard_map/while/body/eval_jaxpr/scatter-add | solution.py:37
  168.3 30.7 %all_to_all.10 = bf16[16,128,256]{2,1,0:T(8,128)(2,1)S(1)} all-to-all(bf16[16,128,256]{2,1,0:T(8,128)(2,1)S(1)} %convert_element_type.21), channel_id=1, replica_groups=mesh['users'=16,'rep'=2] {'users'}, dimensions={0} | all-to-all | bytes 2097152 | tf_op jit(solution)/shard_map/all_to_all | solution.py:79
  200.4 18.4 %all-reduce.3.cloned.1.call-done = (f32[1024,256]{1,0:T(8,128)}, f32[256,256]{1,0:T(8,128)}) async-done(((f32[1024,256]{1,0:T(8,128)}, f32[256,256]{1,0:T(8,128)}), (f32[1024,256]{1,0:T(8,128)}, f32[256,256]{1,0:T(8,128)})) %all-reduce.3.cloned.1.call-update) | async-done | bytes 1310736 | tf_op jit(solution)/shard_map/psum | solution.py:87
  (77 shorter events, 43.7 us)
Async XLA Ops:
  8.8 10.5 %copy-start.10 = (s32[1,1,128]{2,1,0:T(1,128)S(1)}, s32[1,1,128]{2,1,0:T(1,128)}, u32[]{:S(2)}) copy-start(s32[1,1,128]{2,1,0:T(1,128)} %param.15) | copy-start | bytes 1540
  8.8 11.2 %copy-start.11 = (s32[1,1,128]{2,1,0:T(1,128)S(1)}, s32[1,1,128]{2,1,0:T(1,128)}, u32[]{:S(2)}) copy-start(s32[1,1,128]{2,1,0:T(1,128)} %param.16) | copy-start | bytes 1540
  8.8 12.0 %copy-start.4 = (f32[1024,256]{1,0:T(8,128)S(1)}, f32[1024,256]{1,0:T(8,128)}, u32[]{:S(2)}) copy-start(f32[1024,256]{1,0:T(8,128)} %param.10) | copy-start | bytes 3145732
  10.4 32.7 %all-to-all-start = ((bf16[16,128,256]{2,1,0:T(8,128)(2,1)}), bf16[16,128,256]{2,1,0:T(8,128)(2,1)S(1)}, u32[]{:S(2)}, u32[]{:S(2)}) async-start(bf16[16,128,256]{2,1,0:T(8,128)(2,1)} %gather_fusion.2), calls=%async_computation | async-start | bytes 2097152 | tf_op jit(solution)/shard_map/all_to_all | solution.py:75
  18.8 200.1 %all-reduce.3.cloned.1.call-start = ((), (), s32[]{:S(2)}) async-start(), calls=%async_computation.2 | async-start | bytes 2621440 | tf_op jit(solution)/shard_map/psum | solution.py:87
  43.2 1.0 copy-start.2
  50.8 4.4 %copy-start.1 = (bf16[32,128,256]{2,1,0:T(8,128)(2,1)S(1)}, bf16[32,128,256]{2,1,0:T(8,128)(2,1)}, u32[]{:S(2)}) copy-start(bf16[32,128,256]{2,1,0:T(8,128)(2,1)} %gather_fusion) | copy-start | bytes 6291460 | tf_op jit(solution)/shard_map/while
  54.2 1.0 copy-start.3
  81.7 4.4 %copy-start.1 = (bf16[32,128,256]{2,1,0:T(8,128)(2,1)S(1)}, bf16[32,128,256]{2,1,0:T(8,128)(2,1)}, u32[]{:S(2)}) copy-start(bf16[32,128,256]{2,1,0:T(8,128)(2,1)} %gather_fusion) | copy-start | bytes 6291460 | tf_op jit(solution)/shard_map/while
  85.1 1.0 copy-start.3
  112.6 4.4 %copy-start.1 = (bf16[32,128,256]{2,1,0:T(8,128)(2,1)S(1)}, bf16[32,128,256]{2,1,0:T(8,128)(2,1)}, u32[]{:S(2)}) copy-start(bf16[32,128,256]{2,1,0:T(8,128)(2,1)} %gather_fusion) | copy-start | bytes 6291460 | tf_op jit(solution)/shard_map/while
  116.0 1.0 copy-start.3
  143.6 4.4 %copy-start.1 = (bf16[32,128,256]{2,1,0:T(8,128)(2,1)S(1)}, bf16[32,128,256]{2,1,0:T(8,128)(2,1)}, u32[]{:S(2)}) copy-start(bf16[32,128,256]{2,1,0:T(8,128)(2,1)} %gather_fusion) | copy-start | bytes 6291460 | tf_op jit(solution)/shard_map/while
  147.0 1.0 copy-start.3
  168.1 30.8 %copy-start = (f32[8,128,256]{2,1,0:T(8,128)}, f32[8,128,256]{2,1,0:T(8,128)S(1)}, u32[]{:S(2)}) copy-start(f32[8,128,256]{2,1,0:T(8,128)S(1)} %get-tuple-element.69) | copy-start | bytes 3145732
  168.2 30.8 %copy-start.9 = (s32[1,1,16]{2,1,0:T(1,128)S(1)}, s32[1,1,16]{2,1,0:T(1,128)}, u32[]{:S(2)}) copy-start(s32[1,1,16]{2,1,0:T(1,128)} %param.17) | copy-start | bytes 196
  199.0 19.9 %copy-start.7 = (f32[256,256]{1,0:T(8,128)S(1)}, f32[256,256]{1,0:T(8,128)}, u32[]{:S(2)}) copy-start(f32[256,256]{1,0:T(8,128)} %param.12) | copy-start | bytes 786436
  199.0 19.9 %copy-start.8 = (f32[256,256]{1,0:T(8,128)S(1)}, f32[256,256]{1,0:T(8,128)}, u32[]{:S(2)}) copy-start(f32[256,256]{1,0:T(8,128)} %param.13) | copy-start | bytes 786436
  199.0 21.6 %copy-start.5 = (f32[1024,256]{1,0:T(8,128)S(1)}, f32[1024,256]{1,0:T(8,128)}, u32[]{:S(2)}) copy-start(f32[1024,256]{1,0:T(8,128)} %param.10) | copy-start | bytes 3145732
  199.0 21.6 %copy-start.6 = (f32[1024,256]{1,0:T(8,128)S(1)}, f32[1024,256]{1,0:T(8,128)}, u32[]{:S(2)}) copy-start(f32[1024,256]{1,0:T(8,128)} %param.11) | copy-start | bytes 3145732
Sparse Core Ops, SparseCore 0:
  200.6 18.2 all-reduce.2
where the time goes:
time: 232 us; the launch traced here: 230 us
  other arithmetic  60.3 us (26%)
  matrix products  43.3 us (19%)
  waiting for transfers between devices  39.9 us (17%)
  local copies, waits for them, and re-layouts  33.3 us (14%)
  blocking collectives  30.7 us (13%)
  between operations  14.1 us (6%)
  starting transfers between devices  8.38 us (4%)
    all_to_all x1, blocking collectives, local(): lax.all_to_all(slot_part.astype(jnp.bfloat16), 'users', split_axis=0, con...  30.7 us
    scatter-add x4, other arithmetic, tile_step(): slot_total = slot_total.at[block_slot].add(item_part)  25.9 us
    scatter-add x4, other arithmetic, tile_step(): user_total = user_total.at[block_user].add(user_part)  25.8 us
    all_to_all x1, waiting for transfers between devices, local(): lax.all_to_all(outgoing, 'users', split_axis=0, concat_axis=0, tiled=True)  21.4 us
    psum x1, waiting for transfers between devices, local(): user_grad = lax.psum(user_part.reshape(-1, feat_width), 'rep')  18.4 us
    dot_general x4, matrix products, tile_step(): jnp.einsum('gui,gir->gur', weighted_err, item_rows, preferred_element_typ...  18.2 us
    dot_general x4, matrix products, tile_step(): jnp.einsum('gur,gir->gui', user_rows, item_rows, preferred_element_type=j...  13.6 us
    gather x4, local copies, waits for them, and re-layouts, tile_step(): item_rows = panels[block_fetch]  12.9 us
  transfers between devices with their start and end apart: 2, of which 2 were waited for; matrix products, arithmetic and copies ran while one was open for 1% of the time, Pallas kernels for 0%

commit v1 on v0

--- a/solution.py
+++ b/solution.py
@@ -1,12 +1,21 @@
+import functools
 import math
 
 import jax
 import jax.numpy as jnp
 from jax import lax
+from jax.experimental import pallas as pl
+from jax.experimental.pallas import tpu as pltpu
 from jax.sharding import PartitionSpec as P
+
 
 CONF_SLOPE = 0.5
 ERR_SCALE = 1.0 / 64.0
+DENSE_LIMIT = 32 * 1024 * 1024
+TABLE_VMEM = 24 * 1024 * 1024
+GRAD_VMEM = 32 * 1024 * 1024
+TWO_PART = True
+GROUP = 4
 
 
 def tile_terms(user_strip, panels, counts, users_idx, fetch_index, slot_index, slot_count):
@@ -57,7 +66,7 @@
     return (factors - grad / jnp.sqrt(new_accum), new_accum)
 
 
-def local(
+def local_tiles(
     user_factors, user_accum, item_factors, item_accum, tile_counts, tile_user, tile_item, send_list
 ):
     tile_size = tile_counts.shape[-1]
@@ -91,7 +100,345 @@
     return (new_users, new_user_accum, new_items, new_item_accum)
 
 
+def combine_kernel(own, par, out, sems):
+    tiles = own.shape[0]
+    first = pltpu.make_async_copy(own, out.at[pl.ds(0, tiles)], sems.at[0])
+    second = pltpu.make_async_copy(par, out.at[pl.ds(tiles, tiles)], sems.at[1])
+    first.start()
+    second.start()
+    first.wait()
+    second.wait()
+
+
+def combine(own, par):
+    tiles, side, _ = own.shape
+    anywhere = pl.BlockSpec(memory_space=pl.ANY)
+    return pl.pallas_call(
+        combine_kernel,
+        out_shape=jax.ShapeDtypeStruct((2 * tiles, side, side), own.dtype),
+        in_specs=[anywhere, anywhere],
+        out_specs=anywhere,
+        scratch_shapes=[pltpu.SemaphoreType.DMA((2,))],
+        compiler_params=pltpu.CompilerParams(vmem_limit_bytes=TABLE_VMEM),
+        name="combine",
+    )(own, par)
+
+
+def table_kernel(order, begin, counts, s_ref, n_ref):
+    step = pl.program_id(0)
+    side = s_ref.shape[-1]
+    blocks = s_ref.shape[1] // side
+
+    def block(ub, _):
+        pair = step * blocks + ub
+        first, end = begin[pair], begin[pair + 1]
+        rows = pl.ds(pl.multiple_of(ub * side, side), side)
+
+        def terms(k):
+            count = counts[order[k]]
+            hit = jnp.where(count > 0, jnp.bfloat16(ERR_SCALE), jnp.bfloat16(0.0))
+            return count.astype(jnp.float32) * (CONF_SLOPE * ERR_SCALE), hit
+
+        @pl.when(first == end)
+        def _():
+            s_ref[0, rows, :] = jnp.zeros((side, side), jnp.float32)
+            n_ref[0, rows, :] = jnp.zeros((side, side), jnp.bfloat16)
+
+        @pl.when(first < end)
+        def _():
+            half, hit = terms(first)
+            s_ref[0, rows, :] = half
+            n_ref[0, rows, :] = hit
+
+        def more(k, _):
+            half, hit = terms(k)
+            s_ref[0, rows, :] += half
+            n_ref[0, rows, :] += hit
+            return 0
+
+        lax.fori_loop(first + 1, end, more, 0)
+        return 0
+
+    lax.fori_loop(0, blocks, block, 0)
+
+
+def block_tables(order, begin, counts, positions, blocks):
+    side = counts.shape[-1]
+    spec = pl.BlockSpec((1, blocks * side, side), lambda j: (j, 0, 0))
+    shape = (positions, blocks * side, side)
+    scalars = pl.BlockSpec(memory_space=pltpu.SMEM)
+    return pl.pallas_call(
+        table_kernel,
+        grid=(positions,),
+        out_shape=(
+            jax.ShapeDtypeStruct(shape, jnp.float32),
+            jax.ShapeDtypeStruct(shape, jnp.bfloat16),
+        ),
+        in_specs=[scalars, scalars, pl.BlockSpec(memory_space=pltpu.VMEM)],
+        out_specs=(spec, spec),
+        compiler_params=pltpu.CompilerParams(vmem_limit_bytes=TABLE_VMEM),
+        name="tables",
+    )(order, begin, counts)
+
+
+def prepare_kernel(f_ref, u_ref, ut_ref):
+    rounded = f_ref[...].astype(jnp.bfloat16)
+    u_ref[...] = rounded
+    ut_ref[...] = f_ref[...].T.astype(jnp.bfloat16)
+
+
+def prepare_users(factors):
+    strip, width = factors.shape
+    step = math.gcd(strip, 512)
+    return pl.pallas_call(
+        prepare_kernel,
+        grid=(strip // step,),
+        out_shape=(
+            jax.ShapeDtypeStruct((strip, width), jnp.bfloat16),
+            jax.ShapeDtypeStruct((width, strip), jnp.bfloat16),
+        ),
+        in_specs=[pl.BlockSpec((step, width), lambda j: (j, 0))],
+        out_specs=(
+            pl.BlockSpec((step, width), lambda j: (j, 0)),
+            pl.BlockSpec((width, step), lambda j: (0, j)),
+        ),
+        compiler_params=pltpu.CompilerParams(vmem_limit_bytes=GRAD_VMEM),
+        name="prepare",
+    )(factors)
+
+
+def grad_kernel(group, first, tiles_in, u_ref, ut_ref, v_ref, s_ref, n_ref, *refs):
+    if first:
+        g_ref, p_ref = refs
+    else:
+        gin_ref, g_ref, p_ref = refs
+    step = pl.program_id(0)
+    side = s_ref.shape[-1]
+    users = u_ref.shape[0]
+    blocks = users // side
+
+    @pl.when(step == 0)
+    def _():
+        g_ref[...] = jnp.zeros_like(g_ref) if first else gin_ref[...]
+
+    panel = v_ref[...].reshape(group * side, v_ref.shape[-1])
+    predicted = lax.dot_general(
+        u_ref[...], panel, (((1,), (1,)), ((), ())), preferred_element_type=jnp.float32
+    )
+
+    columns, rests = [], []
+    for k in range(group):
+        rows, low = [], []
+        for ub in range(blocks):
+            weight = tiles_in[(step * group + k) * blocks + ub]
+            part = slice(ub * side, (ub + 1) * side)
+            half = s_ref[k, part, :]
+            hits = n_ref[k, part, :].astype(jnp.float32)
+            guess = predicted[part, k * side : (k + 1) * side]
+            err = (weight + half) * guess - (hits + half)
+            rows.append(err.astype(jnp.bfloat16))
+            if TWO_PART:
+                low.append((err - rows[-1].astype(jnp.float32)).astype(jnp.bfloat16))
+        columns.append(jnp.concatenate(rows, axis=0))
+        if TWO_PART:
+            rests.append(jnp.concatenate(low, axis=0))
+    err = jnp.concatenate(columns, axis=1)
+    total = jnp.dot(err, panel, preferred_element_type=jnp.float32)
+    item = jnp.dot(ut_ref[...], err, preferred_element_type=jnp.float32)
+    if TWO_PART:
+        rest = jnp.concatenate(rests, axis=1)
+        total += jnp.dot(rest, panel, preferred_element_type=jnp.float32)
+        item += jnp.dot(ut_ref[...], rest, preferred_element_type=jnp.float32)
+    g_ref[...] += total
+    for k in range(group):
+        p_ref[k] = item[:, k * side : (k + 1) * side].astype(p_ref.dtype)
+
+
+def gradients(tiles_in, users, users_t, panels, s_tab, n_tab, g_in, out_dtype):
+    count, side, width = panels.shape
+    strip = users.shape[0]
+    group = math.gcd(count, GROUP)
+    first = g_in is None
+    whole = pl.BlockSpec((strip, width), lambda j: (0, 0))
+    table = pl.BlockSpec((group, strip, side), lambda j: (j, 0, 0))
+    in_specs = [
+        pl.BlockSpec(memory_space=pltpu.SMEM),
+        whole,
+        pl.BlockSpec((width, strip), lambda j: (0, 0)),
+        pl.BlockSpec((group, side, width), lambda j: (j, 0, 0)),
+        table,
+        table,
+    ]
+    operands = [tiles_in, users, users_t, panels, s_tab, n_tab]
+    if not first:
+        in_specs.append(whole)
+        operands.append(g_in)
+    return pl.pallas_call(
+        functools.partial(grad_kernel, group, first),
+        grid=(count // group,),
+        out_shape=(
+            jax.ShapeDtypeStruct((strip, width), jnp.float32),
+            jax.ShapeDtypeStruct((count, width, side), out_dtype),
+        ),
+        in_specs=in_specs,
+        out_specs=(whole, pl.BlockSpec((group, width, side), lambda j: (j, 0, 0))),
+        compiler_params=pltpu.CompilerParams(vmem_limit_bytes=GRAD_VMEM),
+        name="gradients",
+    )(*operands)
+
+
+def item_kernel(core, here, there, f_ref, a_ref, new_f, new_a):
+    side = here.shape[1]
+    mine = here[...].T
+    theirs = there[...].T
+    for k in range(2):
+        rows = pl.ds(k * side, side)
+        grad = jnp.where(core[0] == k, mine, theirs)
+        total = a_ref[rows, :] + grad * grad
+        new_a[rows, :] = total
+        new_f[rows, :] = f_ref[rows, :] - grad / jnp.sqrt(total)
+
+
+def update_items(core, here, there, factors, accum):
+    vmem = pl.BlockSpec(memory_space=pltpu.VMEM)
+    out = jax.ShapeDtypeStruct(factors.shape, jnp.float32)
+    return pl.pallas_call(
+        item_kernel,
+        out_shape=(out, out),
+        in_specs=[pl.BlockSpec(memory_space=pltpu.SMEM), vmem, vmem, vmem, vmem],
+        out_specs=(vmem, vmem),
+        compiler_params=pltpu.CompilerParams(vmem_limit_bytes=GRAD_VMEM),
+        name="items",
+    )(core.reshape(1), here, there, factors, accum)
+
+
+def in_vmem(x):
+    return pltpu.with_memory_space_constraint(x, pltpu.VMEM)
+
+
+def in_hbm(x):
+    return pltpu.with_memory_space_constraint(x, pltpu.HBM)
+
+
+def local_dense(
+    user_factors, user_accum, item_factors, item_accum, tile_counts, tile_user, tile_item, send_list
+):
+    side = tile_counts.shape[-1]
+    tiles = tile_counts.shape[2]
+    strip, _ = user_factors.shape
+    blocks = strip // side
+    peers = lax.axis_size("users")
+    bits = peers.bit_length() - 1
+    me = lax.axis_index("users")
+    core = lax.axis_index("rep")
+    axes = ("users", "rep")
+
+    order_a = list(range(bits - 1, 1, -1)) + [0, 1]
+    order_b = list(range(bits - 1, 1, -1))[::-1] + [1, 0]
+    stages = list(zip(order_a, order_b))
+
+    def swap(x, *chosen):
+        masks = [sum(1 << stages[s][r] for s in chosen) for r in range(2)]
+        pairs = [(2 * u + r, 2 * (u ^ masks[r]) + r) for u in range(peers) for r in range(2)]
+        return lax.ppermute(x, axes, pairs)
+
+    def other(x):
+        return lax.ppermute(x, "rep", [(0, 1), (1, 0)])
+
+    own_counts = tile_counts[0, 0]
+    mine = lax.dynamic_slice_in_dim(item_factors, core * side, side, 0).astype(jnp.bfloat16)[None]
+    got = swap(mine, 0) if bits > 2 else None
+    code = tile_item[0, 0] * blocks + tile_user[0, 0]
+    codes = jnp.concatenate([code, other(code)])
+    par_counts = other(own_counts)
+    counts = in_vmem(combine(in_hbm(own_counts), in_hbm(par_counts)))
+
+    panel_id = codes // blocks
+    distance = (panel_id // 2) ^ me
+    position = jnp.zeros_like(distance)
+    for s, (bit_a, bit_b) in enumerate(stages):
+        bit = jnp.where(core == 0, bit_a, bit_b)
+        position = position | (((distance >> bit) & 1) << s)
+    pairs = peers * blocks
+    keys = jnp.where(panel_id % 2 == core, position * blocks + codes % blocks, pairs)
+
+    index = jnp.arange(2 * tiles, dtype=jnp.int32)
+    before = (keys[None, :] < keys[:, None]) | (
+        (keys[None, :] == keys[:, None]) & (index[None, :] < index[:, None])
+    )
+    rank = jnp.sum(before.astype(jnp.int32), axis=1)
+    order = jnp.sum(jnp.where(rank[None, :] == index[:, None], index[None, :], 0), axis=1)
+    pair = jnp.arange(pairs + blocks, dtype=jnp.int32)
+    begin = jnp.sum((keys[None, :] < pair[:, None]).astype(jnp.int32), axis=1)
+    weight = (begin[1 : pairs + 1] - begin[:pairs]).astype(jnp.float32) * ERR_SCALE
+
+    span = peers // 4
+
+    def tables(group):
+        part = begin[group * span * blocks : ((group + 1) * span + 1) * blocks]
+        return block_tables(order, part, counts, span, blocks)
+
+    def block_grads(group, panels, table, g_in, out_dtype):
+        weights = weight[group * span * blocks : (group + 1) * span * blocks]
+        return gradients(weights, users, users_t, panels, *table, g_in, out_dtype)
+
+    users, users_t = prepare_users(user_factors)
+    panels = [mine]
+    for s in range(bits - 2):
+        if s:
+            got = swap(panels[0], s)
+        panels[0] = jnp.concatenate([panels[0], got], axis=0)
+    panels.append(swap(panels[0], bits - 2))
+    panels.append(swap(panels[0], bits - 1))
+    panels.append(swap(panels[1], bits - 1))
+
+    table = [tables(group) for group in range(4)]
+
+    grad, send = block_grads(2, panels[2], table[2], None, jnp.bfloat16)
+    got_0 = swap(send, bits - 1)
+    grad, send = block_grads(3, panels[3], table[3], grad, jnp.bfloat16)
+    got_1 = swap(send, bits - 1)
+    grad, keep_1 = block_grads(1, panels[1], table[1], grad, jnp.float32)
+    grad, keep_0 = block_grads(0, panels[0], table[0], grad, jnp.float32)
+
+    send = (keep_1 + got_1.astype(jnp.float32)).astype(jnp.bfloat16)
+    held = keep_0 + got_0.astype(jnp.float32)
+    held = held + swap(send, bits - 2).astype(jnp.float32)
+    grad_there = other(grad)
+    for s in range(bits - 3, 1, -1):
+        span = span // 2
+        held = held[:span] + swap(held[span:], s)
+    parts = []
+    for d in range(span - 1, 0, -1):
+        chosen = [s for s in range(2) if d >> s & 1]
+        parts.append(swap(held[d].astype(jnp.bfloat16), *chosen))
+    here = held[0]
+    for part in parts:
+        here = here + part.astype(jnp.float32)
+
+    new_users, new_user_accum = adagrad(user_factors, user_accum, grad + grad_there)
+
+    there = other(here)
+    new_items, new_item_accum = update_items(core, here, there, item_factors, item_accum)
+    return (new_users, new_user_accum, new_items, new_item_accum)
+
+
 def solution(mesh):
+    peers = mesh.shape["users"]
+
+
+    def local(*args):
+        side = args[4].shape[-1]
+        table_bytes = peers * args[0].shape[0] * side * 2 * 2
+        dense = (
+            mesh.shape["rep"] == 2
+            and args[2].shape[0] == 2 * side
+            and peers >= 4
+            and peers & (peers - 1) == 0
+            and table_bytes <= DENSE_LIMIT
+        )
+        return (local_dense if dense else local_tiles)(*args)
+
     return jax.shard_map(
         local,
         mesh=mesh,

time: 232 us -> 68.3 us (0.29)
  other arithmetic: 60.3 us -> 3.02 us
  matrix products: 43.3 us -> 0 us
  local copies, waits for them, and re-layouts: 33.3 us -> 2.32 us
  blocking collectives: 30.7 us -> 0 us
  waiting for transfers between devices: 39.9 us -> 16.5 us
  Pallas kernels: 0 us -> 21.8 us
  starting transfers between devices: 8.38 us -> 23.6 us
  between operations: 14.1 us -> 0.84 us
    scatter-add x8 -> x0, other arithmetic: 51.7 us -> none  [the longest x4 25.9 us: tile_step(): slot_total = slot_total.at[block_slot].add(item_part)]
    dot_general x13 -> x0, matrix products: 43.3 us -> none  [the longest x4 18.2 us: tile_step(): jnp.einsum('gui,gir->gur', weighted_err, item_rows, preferred_element_typ...]
    all_to_all x1 -> x0, blocking collectives: 30.7 us -> none  [local(): lax.all_to_all(slot_part.astype(jnp.bfloat16), 'users', split_axis=0, con...]
    gather x9 -> x0, local copies, waits for them, and re-layouts: 26.8 us -> none  [the longest x4 12.9 us: tile_step(): item_rows = panels[block_fetch]]
    ppermute x0 -> x15, starting transfers between devices: none -> 23.6 us  [the longest x11 22.8 us: swap(): return lax.ppermute(x, axes, pairs)]
    pallas_call x0 -> x11, Pallas kernels: none -> 21.8 us  [the longest x4 9.19 us: gradients(): pl.pallas_call(functools.partial(grad_kernel, group, first), grid=(count...]
    all_to_all x1 -> x0, waiting for transfers between devices: 21.4 us -> none  [local(): lax.all_to_all(outgoing, 'users', split_axis=0, concat_axis=0, tiled=True)]
    psum x1 -> x0, waiting for transfers between devices: 18.4 us -> none  [local(): user_grad = lax.psum(user_part.reshape(-1, feat_width), 'rep')]
  transfers between devices with their start and end apart: 2 -> 15, of which waited for: 2 -> 7; matrix products, arithmetic and copies ran while one was open for 1% -> 4% of each run, Pallas kernels for 0% -> 29%
where the time goes in v1:
time: 68.3 us; the launch traced here: 68.1 us
  starting transfers between devices  23.6 us (35%)
  Pallas kernels  21.8 us (32%)
  waiting for transfers between devices  16.5 us (24%)
  other arithmetic  3.02 us (4%)
  local copies, waits for them, and re-layouts  2.32 us (3%)
  between operations  0.84 us (1%)
    ppermute x11, starting transfers between devices, swap(): return lax.ppermute(x, axes, pairs)  22.8 us
    ppermute x11, waiting for transfers between devices, swap(): return lax.ppermute(x, axes, pairs)  15.2 us
    pallas_call x4, Pallas kernels, gradients(): pl.pallas_call(functools.partial(grad_kernel, group, first), grid=(count...  9.19 us
    pallas_call x4, Pallas kernels, block_tables(): pl.pallas_call(table_kernel, grid=(positions,), out_shape=(jax.ShapeDtype...  7.78 us
    pallas_call x1, Pallas kernels, combine(): pl.pallas_call(combine_kernel, out_shape=jax.ShapeDtypeStruct((2 * tiles,...  3.49 us
    sub x1, other arithmetic, adagrad(): return (factors - grad / jnp.sqrt(new_accum), new_accum)  1.59 us
  transfers between devices with their start and end apart: 15, of which 7 were waited for; matrix products, arithmetic and copies ran while one was open for 4% of the time, Pallas kernels for 29%

profile of v1, /device:TPU:0, one launch (start us, length us, event | category | flops | bytes accessed | tf_op | source)
XLA Modules:
  0.0 68.1 jit_solution(1327102091061039327)
XLA Ops:
  2.8 4.1 %collective-permute-start.1 = (bf16[1,128,256]{2,1,0:T(8,128)(2,1)S(1)}, bf16[1,128,256]{2,1,0:T(8,128)(2,1)S(1)}, u32[]{:S(2)}, u32[]{:S(2)}) collective-permute-start(bf16[1,128,256]{2,1,0:T(8,128)(2,1)S(1)} %fusion.5), channel_id=1, source_target_pairs={{0,16},{1,9},{2,18},{3,11},{4,20},{5,13},{6,22},{7,15},{8,24},{9,1... | collective-permute-start | bytes 196616 | tf_op jit(solution)/shard_map/ppermute | solution.py:343
  9.2 2.3 %collective-permute-start.2 = (bf16[2,128,256]{2,1,0:T(8,128)(2,1)S(1)}, bf16[2,128,256]{2,1,0:T(8,128)(2,1)S(1)}, u32[]{:S(2)}, u32[]{:S(2)}) collective-permute-start(bf16[2,128,256]{2,1,0:T(8,128)(2,1)S(1)} %pad_maximum_fusion.1), channel_id=1, source_target_pairs={{0,8},{1,17},{2,10},{3,19},{4,12},{5,21},{6,14},{7,23},{8,0},{9,25... | collective-permute-start | bytes 393224 | tf_op jit(solution)/shard_map/ppermute | solution.py:343
  11.6 4.0 %collective-permute-done.2 = bf16[2,128,256]{2,1,0:T(8,128)(2,1)S(1)} collective-permute-done((bf16[2,128,256]{2,1,0:T(8,128)(2,1)S(1)}, bf16[2,128,256]{2,1,0:T(8,128)(2,1)S(1)}, u32[]{:S(2)}, u32[]{:S(2)}) %collective-permute-start.2) | collective-permute-done | bytes 131104 | tf_op jit(solution)/shard_map/ppermute | solution.py:343
  15.6 2.2 %collective-permute-start.4 = (bf16[4,128,256]{2,1,0:T(8,128)(2,1)S(1)}, bf16[4,128,256]{2,1,0:T(8,128)(2,1)S(1)}, u32[]{:S(2)}, u32[]{:S(2)}) collective-permute-start(bf16[4,128,256]{2,1,0:T(8,128)(2,1)S(1)} %pad_maximum_fusion.v_ref), channel_id=1, source_target_pairs={{0,2},{1,5},{2,0},{3,7},{4,6},{5,1},{6,4},{7,3},{8,10},{9,13},{10,... | collective-permute-start | bytes 786440 | tf_op jit(solution)/shard_map/ppermute | solution.py:343
  18.1 1.5 %collective-permute-start.6 = (bf16[4,128,256]{2,1,0:T(8,128)(2,1)S(1)}, bf16[4,128,256]{2,1,0:T(8,128)(2,1)S(1)}, u32[]{:S(2)}, u32[]{:S(2)}) collective-permute-start(bf16[4,128,256]{2,1,0:T(8,128)(2,1)S(1)} %pad_maximum_fusion.v_ref), channel_id=1, source_target_pairs={{0,4},{1,3},{2,6},{3,1},{4,0},{5,7},{6,2},{7,5},{8,12},{9,11},{10,... | collective-permute-start | bytes 786440 | tf_op jit(solution)/shard_map/ppermute | solution.py:343
  19.6 4.4 %collective-permute-done.4.v_ref = bf16[4,128,256]{2,1,0:T(8,128)(2,1)S(1)} collective-permute-done((bf16[4,128,256]{2,1,0:T(8,128)(2,1)S(1)}, bf16[4,128,256]{2,1,0:T(8,128)(2,1)S(1)}, u32[]{:S(2)}, u32[]{:S(2)}) %collective-permute-start.4) | collective-permute-done | bytes 262176 | tf_op jit(solution)/shard_map/ppermute | solution.py:343
  24.0 2.4 %collective-permute-start.5 = (bf16[4,128,256]{2,1,0:T(8,128)(2,1)S(1)}, bf16[4,128,256]{2,1,0:T(8,128)(2,1)S(1)}, u32[]{:S(2)}, u32[]{:S(2)}) collective-permute-start(bf16[4,128,256]{2,1,0:T(8,128)(2,1)S(1)} %collective-permute-done.4.v_ref), channel_id=1, source_target_pairs={{0,4},{1,3},{2,6},{3,1},{4,0},{5,7},{6,2},{7,5},{8,12},{9,11},{10,... | collective-permute-start | bytes 786440 | tf_op jit(solution)/shard_map/ppermute | solution.py:343
  26.6 3.5 %combine.1.counts = bf16[256,128,128]{2,1,0:T(8,128)(2,1)S(1)} custom-call(bf16[128,128,128]{2,1,0:T(8,128)(2,1)} %bitcast.21, bf16[128,128,128]{2,1,0:T(8,128)(2,1)} %collective-permute-done.3.par), custom_call_target="tpu_custom_call" | custom-call | tf_op jit(solution)/shard_map/combine/pallas_call | solution.py:116
  30.1 1.9 %tables.7 = (f32[4,1024,128]{2,1,0:T(8,128)S(1)}, bf16[4,1024,128]{2,1,0:T(8,128)(2,1)S(1)}) custom-call(s32[256]{0:T(256)S(1)} %select_reduce_fusion.order, s32[40]{0:T(128)S(1)} %get-tuple-element.51.begin, bf16[256,128,128]{2,1,0:T(8,128)(2,1)S(1)} %combine.1.counts), custom_call_target="tpu_custom_call" | custom-call | tf_op jit(solution)/shard_map/tables/pallas_call | solution.py:170
  32.0 2.1 %tables.6 = (f32[4,1024,128]{2,1,0:T(8,128)S(1)}, bf16[4,1024,128]{2,1,0:T(8,128)(2,1)S(1)}) custom-call(s32[256]{0:T(256)S(1)} %select_reduce_fusion.order, s32[40]{0:T(128)S(1)} %get-tuple-element.52.begin, bf16[256,128,128]{2,1,0:T(8,128)(2,1)S(1)} %combine.1.counts), custom_call_target="tpu_custom_call" | custom-call | tf_op jit(solution)/shard_map/tables/pallas_call | solution.py:170
  34.1 2.3 %gradients.4 = (f32[1024,256]{1,0:T(8,128)S(1)}, bf16[4,256,128]{2,1,0:T(8,128)(2,1)S(1)}) custom-call(f32[32]{0:T(128)S(1)} %get-tuple-element.55.tiles_in, bf16[1024,256]{1,0:T(8,128)(2,1)S(1)} %get-tuple-element.24.u_ref, bf16[256,1024]{1,0:T(8,128)(2,1)S(1)} %get-tuple-element.25.ut_ref, bf16[4,128,256]{2,1,0:T(8,128)(2,1)S(1)} %collective-permute-done.6.v_ref, ...), custom_call_target="tpu_custom_call" | custom-call | tf_op jit(solution)/shard_map/gradients/pallas_call | solution.py:276
  36.4 2.3 %gradients.5 = (f32[1024,256]{1,0:T(8,128)S(1)}, bf16[4,256,128]{2,1,0:T(8,128)(2,1)S(1)}) custom-call(f32[32]{0:T(128)S(1)} %get-tuple-element.56.tiles_in, bf16[1024,256]{1,0:T(8,128)(2,1)S(1)} %get-tuple-element.24.u_ref, bf16[256,1024]{1,0:T(8,128)(2,1)S(1)} %get-tuple-element.25.ut_ref, bf16[4,128,256]{2,1,0:T(8,128)(2,1)S(1)} %collective-permute-done.5.v_ref, ...), custom_call_target="tpu_custom_call" | custom-call | tf_op jit(solution)/shard_map/gradients/pallas_call | solution.py:276
  39.2 1.7 %tables.5 = (f32[4,1024,128]{2,1,0:T(8,128)S(1)}, bf16[4,1024,128]{2,1,0:T(8,128)(2,1)S(1)}) custom-call(s32[256]{0:T(256)S(1)} %select_reduce_fusion.order, s32[40]{0:T(128)S(1)} %get-tuple-element.53.begin, bf16[256,128,128]{2,1,0:T(8,128)(2,1)S(1)} %combine.1.counts), custom_call_target="tpu_custom_call" | custom-call | tf_op jit(solution)/shard_map/tables/pallas_call | solution.py:170
  40.9 2.0 %collective-permute-start.8 = (bf16[4,256,128]{2,1,0:T(8,128)(2,1)S(1)}, bf16[4,256,128]{2,1,0:T(8,128)(2,1)S(1)}, u32[]{:S(2)}, u32[]{:S(2)}) collective-permute-start(bf16[4,256,128]{2,1,0:T(8,128)(2,1)S(1)} %get-tuple-element.39), channel_id=1, source_target_pairs={{0,4},{1,3},{2,6},{3,1},{4,0},{5,7},{6,2},{7,5},{8,12},{9,11},{10,... | collective-permute-start | bytes 786440 | tf_op jit(solution)/shard_map/ppermute | solution.py:343
  42.9 2.3 %gradients.6 = (f32[1024,256]{1,0:T(8,128)S(1)}, f32[4,256,128]{2,1,0:T(8,128)S(1)}) custom-call(f32[32]{0:T(128)S(1)} %get-tuple-element.57.tiles_in, bf16[1024,256]{1,0:T(8,128)(2,1)S(1)} %get-tuple-element.24.u_ref, bf16[256,1024]{1,0:T(8,128)(2,1)S(1)} %get-tuple-element.25.ut_ref, bf16[4,128,256]{2,1,0:T(8,128)(2,1)S(1)} %collective-permute-done.4.v_ref, ...), custom_call_target="tpu_custom_call" | custom-call | tf_op jit(solution)/shard_map/gradients/pallas_call | solution.py:276
  45.2 2.6 %collective-permute-start.10 = (bf16[4,256,128]{2,1,0:T(8,128)(2,1)S(1)}, bf16[4,256,128]{2,1,0:T(8,128)(2,1)S(1)}, u32[]{:S(2)}, u32[]{:S(2)}) collective-permute-start(bf16[4,256,128]{2,1,0:T(8,128)(2,1)S(1)} %add_convert_fusion), channel_id=1, source_target_pairs={{0,2},{1,5},{2,0},{3,7},{4,6},{5,1},{6,4},{7,3},{8,10},{9,13},{10,... | collective-permute-start | bytes 786440 | tf_op jit(solution)/shard_map/ppermute | solution.py:343
  47.9 2.1 %tables.4 = (f32[4,1024,128]{2,1,0:T(8,128)S(1)}, bf16[4,1024,128]{2,1,0:T(8,128)(2,1)S(1)}) custom-call(s32[256]{0:T(256)S(1)} %select_reduce_fusion.order, s32[40]{0:T(128)S(1)} %get-tuple-element.54.begin, bf16[256,128,128]{2,1,0:T(8,128)(2,1)S(1)} %combine.1.counts), custom_call_target="tpu_custom_call" | custom-call | tf_op jit(solution)/shard_map/tables/pallas_call | solution.py:170
  50.0 2.3 %gradients.7 = (f32[1024,256]{1,0:T(8,128)S(1)}, f32[4,256,128]{2,1,0:T(8,128)S(1)}) custom-call(f32[32]{0:T(128)S(1)} %get-tuple-element.58.tiles_in, bf16[1024,256]{1,0:T(8,128)(2,1)S(1)} %get-tuple-element.24.u_ref, bf16[256,1024]{1,0:T(8,128)(2,1)S(1)} %get-tuple-element.25.ut_ref, bf16[4,128,256]{2,1,0:T(8,128)(2,1)S(1)} %pad_maximum_fusion.v_ref, ...), custom_call_target="tpu_custom_call" | custom-call | tf_op jit(solution)/shard_map/gradients/pallas_call | solution.py:276
  52.5 4.6 %collective-permute-start.11 = (bf16[256,128]{1,0:T(8,128)(2,1)S(1)}, bf16[256,128]{1,0:T(8,128)(2,1)S(1)}, u32[]{:S(2)}, u32[]{:S(2)}) collective-permute-start(bf16[256,128]{1,0:T(8,128)(2,1)S(1)} %get-tuple-element.48), channel_id=1, source_target_pairs={{0,24},{1,25},{2,26},{3,27},{4,28},{5,29},{6,30},{7,31},{8,16},{9,... | collective-permute-start | bytes 196616 | tf_op jit(solution)/shard_map/ppermute | solution.py:343
  57.7 2.4 %collective-permute-done.11 = bf16[256,128]{1,0:T(8,128)(2,1)S(1)} collective-permute-done((bf16[256,128]{1,0:T(8,128)(2,1)S(1)}, bf16[256,128]{1,0:T(8,128)(2,1)S(1)}, u32[]{:S(2)}, u32[]{:S(2)}) %collective-permute-start.11) | collective-permute-done | bytes 65568 | tf_op jit(solution)/shard_map/ppermute | solution.py:343
  60.1 1.3 %collective-permute-done.12 = bf16[256,128]{1,0:T(8,128)(2,1)S(1)} collective-permute-done((bf16[256,128]{1,0:T(8,128)(2,1)S(1)}, bf16[256,128]{1,0:T(8,128)(2,1)S(1)}, u32[]{:S(2)}, u32[]{:S(2)}) %collective-permute-start.12) | collective-permute-done | bytes 65568 | tf_op jit(solution)/shard_map/ppermute | solution.py:343
  61.5 2.6 %collective-permute-done.13 = bf16[256,128]{1,0:T(8,128)(2,1)S(1)} collective-permute-done((bf16[256,128]{1,0:T(8,128)(2,1)S(1)}, bf16[256,128]{1,0:T(8,128)(2,1)S(1)}, u32[]{:S(2)}, u32[]{:S(2)}) %collective-permute-start.13) | collective-permute-done | bytes 65568 | tf_op jit(solution)/shard_map/ppermute | solution.py:343
  64.2 1.3 %collective-permute-done.14.there = f32[256,128]{1,0:T(8,128)S(1)} collective-permute-done((f32[256,128]{1,0:T(8,128)S(1)}, f32[256,128]{1,0:T(8,128)S(1)}, u32[]{:S(2)}, u32[]{:S(2)}) %collective-permute-start.14) | collective-permute-done | bytes 131104 | tf_op jit(solution)/shard_map/ppermute | solution.py:346
  66.5 1.6 %multiply_subtract_fusion = (f32[1024,256]{1,0:T(8,128)}, f32[1024,256]{1,0:T(8,128)}) fusion(f32[1024,256]{1,0:T(8,128)S(1)} %copy-done.1, f32[1024,256]{1,0:T(8,128)S(1)} %copy-done.4, f32[1024,256]{1,0:T(8,128)S(1)} %get-tuple-element.37, f32[1024,256]{1,0:T(8,128)S(1)} %collective-permute-done.7), kind=kLoop, calls=%fused_computation | loop fusion | flops 1310720 | bytes 6291456 | tf_op jit(solution)/shard_map/sub | solution.py:66
  (43 shorter events, 7.5 us)
Async XLA Ops:
  0.6 26.0 %collective-permute-start.3 = (bf16[128,128,128]{2,1,0:T(8,128)(2,1)}, bf16[128,128,128]{2,1,0:T(8,128)(2,1)}, u32[]{:S(2)}, u32[]{:S(2)}) collective-permute-start(bf16[128,128,128]{2,1,0:T(8,128)(2,1)} %bitcast.20), channel_id=1, source_target_pairs={{0,1},{1,0},{2,3},{3,2},{4,5},{5,4},{6,7},{7,6},{8,9},{9,8},{10,11... | collective-permute-start | bytes 12582920 | tf_op jit(solution)/shard_map/ppermute | solution.py:346
  1.9 6.6 %collective-permute-start = (s32[128]{0:T(128)S(1)}, s32[128]{0:T(128)S(1)}, u32[]{:S(2)}, u32[]{:S(2)}) collective-permute-start(s32[128]{0:T(128)S(1)} %add_bitcast_fusion), channel_id=1, source_target_pairs={{0,1},{1,0},{2,3},{3,2},{4,5},{5,4},{6,7},{7,6},{8,9},{9,8},{10,11... | collective-permute-start | bytes 1544 | tf_op jit(solution)/shard_map/ppermute | solution.py:346
  2.8 6.4 %collective-permute-start.1 = (bf16[1,128,256]{2,1,0:T(8,128)(2,1)S(1)}, bf16[1,128,256]{2,1,0:T(8,128)(2,1)S(1)}, u32[]{:S(2)}, u32[]{:S(2)}) collective-permute-start(bf16[1,128,256]{2,1,0:T(8,128)(2,1)S(1)} %fusion.5), channel_id=1, source_target_pairs={{0,16},{1,9},{2,18},{3,11},{4,20},{5,13},{6,22},{7,15},{8,24},{9,1... | collective-permute-start | bytes 196616 | tf_op jit(solution)/shard_map/ppermute | solution.py:343
  6.9 1.2 %copy-start = (f32[1024,256]{1,0:T(8,128)S(1)}, f32[1024,256]{1,0:T(8,128)}, u32[]{:S(2)}) copy-start(f32[1024,256]{1,0:T(8,128)} %f_ref.2) | copy-start | bytes 3145732
  9.2 6.4 %collective-permute-start.2 = (bf16[2,128,256]{2,1,0:T(8,128)(2,1)S(1)}, bf16[2,128,256]{2,1,0:T(8,128)(2,1)S(1)}, u32[]{:S(2)}, u32[]{:S(2)}) collective-permute-start(bf16[2,128,256]{2,1,0:T(8,128)(2,1)S(1)} %pad_maximum_fusion.1), channel_id=1, source_target_pairs={{0,8},{1,17},{2,10},{3,19},{4,12},{5,21},{6,14},{7,23},{8,0},{9,25... | collective-permute-start | bytes 393224 | tf_op jit(solution)/shard_map/ppermute | solution.py:343
  15.6 8.4 %collective-permute-start.4 = (bf16[4,128,256]{2,1,0:T(8,128)(2,1)S(1)}, bf16[4,128,256]{2,1,0:T(8,128)(2,1)S(1)}, u32[]{:S(2)}, u32[]{:S(2)}) collective-permute-start(bf16[4,128,256]{2,1,0:T(8,128)(2,1)S(1)} %pad_maximum_fusion.v_ref), channel_id=1, source_target_pairs={{0,2},{1,5},{2,0},{3,7},{4,6},{5,1},{6,4},{7,3},{8,10},{9,13},{10,... | collective-permute-start | bytes 786440 | tf_op jit(solution)/shard_map/ppermute | solution.py:343
  18.1 16.0 %collective-permute-start.6 = (bf16[4,128,256]{2,1,0:T(8,128)(2,1)S(1)}, bf16[4,128,256]{2,1,0:T(8,128)(2,1)S(1)}, u32[]{:S(2)}, u32[]{:S(2)}) collective-permute-start(bf16[4,128,256]{2,1,0:T(8,128)(2,1)S(1)} %pad_maximum_fusion.v_ref), channel_id=1, source_target_pairs={{0,4},{1,3},{2,6},{3,1},{4,0},{5,7},{6,2},{7,5},{8,12},{9,11},{10,... | collective-permute-start | bytes 786440 | tf_op jit(solution)/shard_map/ppermute | solution.py:343
  24.0 12.4 %collective-permute-start.5 = (bf16[4,128,256]{2,1,0:T(8,128)(2,1)S(1)}, bf16[4,128,256]{2,1,0:T(8,128)(2,1)S(1)}, u32[]{:S(2)}, u32[]{:S(2)}) collective-permute-start(bf16[4,128,256]{2,1,0:T(8,128)(2,1)S(1)} %collective-permute-done.4.v_ref), channel_id=1, source_target_pairs={{0,4},{1,3},{2,6},{3,1},{4,0},{5,7},{6,2},{7,5},{8,12},{9,11},{10,... | collective-permute-start | bytes 786440 | tf_op jit(solution)/shard_map/ppermute | solution.py:343
  38.7 6.4 %collective-permute-start.9 = (bf16[4,256,128]{2,1,0:T(8,128)(2,1)S(1)}, bf16[4,256,128]{2,1,0:T(8,128)(2,1)S(1)}, u32[]{:S(2)}, u32[]{:S(2)}) collective-permute-start(bf16[4,256,128]{2,1,0:T(8,128)(2,1)S(1)} %get-tuple-element.41), channel_id=1, source_target_pairs={{0,4},{1,3},{2,6},{3,1},{4,0},{5,7},{6,2},{7,5},{8,12},{9,11},{10,... | collective-permute-start | bytes 786440 | tf_op jit(solution)/shard_map/ppermute | solution.py:343
  40.9 11.5 %collective-permute-start.8 = (bf16[4,256,128]{2,1,0:T(8,128)(2,1)S(1)}, bf16[4,256,128]{2,1,0:T(8,128)(2,1)S(1)}, u32[]{:S(2)}, u32[]{:S(2)}) collective-permute-start(bf16[4,256,128]{2,1,0:T(8,128)(2,1)S(1)} %get-tuple-element.39), channel_id=1, source_target_pairs={{0,4},{1,3},{2,6},{3,1},{4,0},{5,7},{6,2},{7,5},{8,12},{9,11},{10,... | collective-permute-start | bytes 786440 | tf_op jit(solution)/shard_map/ppermute | solution.py:343
  45.2 7.2 %collective-permute-start.10 = (bf16[4,256,128]{2,1,0:T(8,128)(2,1)S(1)}, bf16[4,256,128]{2,1,0:T(8,128)(2,1)S(1)}, u32[]{:S(2)}, u32[]{:S(2)}) collective-permute-start(bf16[4,256,128]{2,1,0:T(8,128)(2,1)S(1)} %add_convert_fusion), channel_id=1, source_target_pairs={{0,2},{1,5},{2,0},{3,7},{4,6},{5,1},{6,4},{7,3},{8,10},{9,13},{10,... | collective-permute-start | bytes 786440 | tf_op jit(solution)/shard_map/ppermute | solution.py:343
  52.3 13.2 %copy-start.2 = (f32[256,256]{1,0:T(8,128)S(1)}, f32[256,256]{1,0:T(8,128)}, u32[]{:S(2)}) copy-start(f32[256,256]{1,0:T(8,128)} %f_ref.3) | copy-start | bytes 786436
  52.3 13.2 %copy-start.3 = (f32[256,256]{1,0:T(8,128)S(1)}, f32[256,256]{1,0:T(8,128)}, u32[]{:S(2)}) copy-start(f32[256,256]{1,0:T(8,128)} %a_ref.1) | copy-start | bytes 786436
  52.3 14.2 %copy-start.1 = (f32[1024,256]{1,0:T(8,128)S(1)}, f32[1024,256]{1,0:T(8,128)}, u32[]{:S(2)}) copy-start(f32[1024,256]{1,0:T(8,128)} %f_ref.2) | copy-start | bytes 3145732
  52.3 14.2 %copy-start.4 = (f32[1024,256]{1,0:T(8,128)S(1)}, f32[1024,256]{1,0:T(8,128)}, u32[]{:S(2)}) copy-start(f32[1024,256]{1,0:T(8,128)} %param.9) | copy-start | bytes 3145732
  52.3 14.2 %collective-permute-start.7 = (f32[1024,256]{1,0:T(8,128)S(1)}, f32[1024,256]{1,0:T(8,128)S(1)}, u32[]{:S(2)}, u32[]{:S(2)}) collective-permute-start(f32[1024,256]{1,0:T(8,128)S(1)} %get-tuple-element.37), channel_id=1, source_target_pairs={{0,1},{1,0},{2,3},{3,2},{4,5},{5,4},{6,7},{7,6},{8,9},{9,8},{10,11... | collective-permute-start | bytes 3145736 | tf_op jit(solution)/shard_map/ppermute | solution.py:346
  52.5 7.6 %collective-permute-start.11 = (bf16[256,128]{1,0:T(8,128)(2,1)S(1)}, bf16[256,128]{1,0:T(8,128)(2,1)S(1)}, u32[]{:S(2)}, u32[]{:S(2)}) collective-permute-start(bf16[256,128]{1,0:T(8,128)(2,1)S(1)} %get-tuple-element.48), channel_id=1, source_target_pairs={{0,24},{1,25},{2,26},{3,27},{4,28},{5,29},{6,30},{7,31},{8,16},{9,... | collective-permute-start | bytes 196616 | tf_op jit(solution)/shard_map/ppermute | solution.py:343
  57.1 4.4 %collective-permute-start.12 = (bf16[256,128]{1,0:T(8,128)(2,1)S(1)}, bf16[256,128]{1,0:T(8,128)(2,1)S(1)}, u32[]{:S(2)}, u32[]{:S(2)}) collective-permute-start(bf16[256,128]{1,0:T(8,128)(2,1)S(1)} %get-tuple-element.50), channel_id=1, source_target_pairs={{0,8},{1,17},{2,10},{3,19},{4,12},{5,21},{6,14},{7,23},{8,0},{9,25... | collective-permute-start | bytes 196616 | tf_op jit(solution)/shard_map/ppermute | solution.py:343
  57.1 6.9 %collective-permute-start.13 = (bf16[256,128]{1,0:T(8,128)(2,1)S(1)}, bf16[256,128]{1,0:T(8,128)(2,1)S(1)}, u32[]{:S(2)}, u32[]{:S(2)}) collective-permute-start(bf16[256,128]{1,0:T(8,128)(2,1)S(1)} %get-tuple-element.49), channel_id=1, source_target_pairs={{0,16},{1,9},{2,18},{3,11},{4,20},{5,13},{6,22},{7,15},{8,24},{9,1... | collective-permute-start | bytes 196616 | tf_op jit(solution)/shard_map/ppermute | solution.py:343
  64.1 1.4 %collective-permute-start.14 = (f32[256,128]{1,0:T(8,128)S(1)}, f32[256,128]{1,0:T(8,128)S(1)}, u32[]{:S(2)}, u32[]{:S(2)}) collective-permute-start(f32[256,128]{1,0:T(8,128)S(1)} %fusion.4.here), channel_id=1, source_target_pairs={{0,1},{1,0},{2,3},{3,2},{4,5},{5,4},{6,7},{7,6},{8,9},{9,8},{10,11... | collective-permute-start | bytes 393224 | tf_op jit(solution)/shard_map/ppermute | solution.py:346

commit v2 on v1

--- a/solution.py
+++ b/solution.py
@@ -100,14 +100,18 @@
     return (new_users, new_user_accum, new_items, new_item_accum)
 
 
-def combine_kernel(own, par, out, sems):
+def combine_kernel(own, par, out, zeros, sems):
     tiles = own.shape[0]
-    first = pltpu.make_async_copy(own, out.at[pl.ds(0, tiles)], sems.at[0])
-    second = pltpu.make_async_copy(par, out.at[pl.ds(tiles, tiles)], sems.at[1])
-    first.start()
-    second.start()
-    first.wait()
-    second.wait()
+    zeros[...] = jnp.zeros_like(zeros)
+    copies = [
+        pltpu.make_async_copy(own, out.at[pl.ds(0, tiles)], sems.at[0]),
+        pltpu.make_async_copy(par, out.at[pl.ds(tiles, tiles)], sems.at[1]),
+        pltpu.make_async_copy(zeros, out.at[pl.ds(2 * tiles, 1)], sems.at[2]),
+    ]
+    for copy in copies:
+        copy.start()
+    for copy in copies:
+        copy.wait()
 
 
 def combine(own, par):
@@ -115,67 +119,71 @@
     anywhere = pl.BlockSpec(memory_space=pl.ANY)
     return pl.pallas_call(
         combine_kernel,
-        out_shape=jax.ShapeDtypeStruct((2 * tiles, side, side), own.dtype),
+        out_shape=jax.ShapeDtypeStruct((2 * tiles + 1, side, side), own.dtype),
         in_specs=[anywhere, anywhere],
         out_specs=anywhere,
-        scratch_shapes=[pltpu.SemaphoreType.DMA((2,))],
+        scratch_shapes=[
+            pltpu.VMEM((1, side, side), own.dtype),
+            pltpu.SemaphoreType.DMA((3,)),
+        ],
         compiler_params=pltpu.CompilerParams(vmem_limit_bytes=TABLE_VMEM),
         name="combine",
     )(own, par)
 
 
 def table_kernel(order, begin, counts, s_ref, n_ref):
-    step = pl.program_id(0)
-    side = s_ref.shape[-1]
-    blocks = s_ref.shape[1] // side
-
-    def block(ub, _):
-        pair = step * blocks + ub
-        first, end = begin[pair], begin[pair + 1]
-        rows = pl.ds(pl.multiple_of(ub * side, side), side)
-
-        def terms(k):
-            count = counts[order[k]]
-            hit = jnp.where(count > 0, jnp.bfloat16(ERR_SCALE), jnp.bfloat16(0.0))
-            return count.astype(jnp.float32) * (CONF_SLOPE * ERR_SCALE), hit
-
-        @pl.when(first == end)
-        def _():
-            s_ref[0, rows, :] = jnp.zeros((side, side), jnp.float32)
-            n_ref[0, rows, :] = jnp.zeros((side, side), jnp.bfloat16)
-
-        @pl.when(first < end)
-        def _():
-            half, hit = terms(first)
-            s_ref[0, rows, :] = half
-            n_ref[0, rows, :] = hit
-
-        def more(k, _):
-            half, hit = terms(k)
-            s_ref[0, rows, :] += half
-            n_ref[0, rows, :] += hit
+    positions, strip, side = s_ref.shape
+    blocks = strip // side
+    last = order.shape[0] - 1
+    empty = counts.shape[0] - 1
+
+    def terms(tile):
+        count = counts[tile]
+        hit = jnp.where(count > 0, jnp.bfloat16(ERR_SCALE), jnp.bfloat16(0.0))
+        return count.astype(jnp.float32) * (CONF_SLOPE * ERR_SCALE), hit
+
+    def position(step, _):
+        for ub in range(blocks):
+            pair = step * blocks + ub
+            rows = slice(ub * side, (ub + 1) * side)
+            first = begin[pair]
+            used = first < begin[pair + 1]
+            half, hit = terms(jnp.where(used, order[jnp.minimum(first, last)], empty))
+            s_ref[step, rows, :] = half
+            n_ref[step, rows, :] = hit
+
+        def block(ub, _):
+            pair = step * blocks + ub
+            rows = pl.ds(pl.multiple_of(ub * side, side), side)
+
+            def more(k, _):
+                half, hit = terms(order[k])
+                s_ref[step, rows, :] += half
+                n_ref[step, rows, :] += hit
+                return 0
+
+            lax.fori_loop(begin[pair] + 1, begin[pair + 1], more, 0)
             return 0
 
-        lax.fori_loop(first + 1, end, more, 0)
+        lax.fori_loop(0, blocks, block, 0)
         return 0
 
-    lax.fori_loop(0, blocks, block, 0)
+    lax.fori_loop(0, positions, position, 0)
 
 
 def block_tables(order, begin, counts, positions, blocks):
     side = counts.shape[-1]
-    spec = pl.BlockSpec((1, blocks * side, side), lambda j: (j, 0, 0))
     shape = (positions, blocks * side, side)
     scalars = pl.BlockSpec(memory_space=pltpu.SMEM)
+    whole = pl.BlockSpec(memory_space=pltpu.VMEM)
     return pl.pallas_call(
         table_kernel,
-        grid=(positions,),
         out_shape=(
             jax.ShapeDtypeStruct(shape, jnp.float32),
             jax.ShapeDtypeStruct(shape, jnp.bfloat16),
         ),
-        in_specs=[scalars, scalars, pl.BlockSpec(memory_space=pltpu.VMEM)],
-        out_specs=(spec, spec),
+        in_specs=[scalars, scalars, whole],
+        out_specs=(whole, whole),
         compiler_params=pltpu.CompilerParams(vmem_limit_bytes=TABLE_VMEM),
         name="tables",
     )(order, begin, counts)

time: 68.3 us -> 66.7 us (0.977)
  Pallas kernels: 21.8 us -> 20.8 us
  waiting for transfers between devices: 16.5 us -> 15.6 us
    pallas_call x5, Pallas kernels: 11.3 us -> 10.3 us  [the longest x4 6.79 us: block_tables(): pl.pallas_call(table_kernel, out_shape=(jax.ShapeDtypeStruct(shape, jnp.f...]
    ppermute x11, waiting for transfers between devices: 15.2 us -> 14.3 us  [swap(): return lax.ppermute(x, axes, pairs)]
  transfers between devices with their start and end apart: 15 -> 15, of which waited for: 7 -> 9; matrix products, arithmetic and copies ran while one was open for 4% -> 4% of each run, Pallas kernels for 29% -> 28%
where the time goes in v2:
time: 66.7 us; the launch traced here: 66.5 us
  starting transfers between devices  23.9 us (36%)
  Pallas kernels  20.8 us (31%)
  waiting for transfers between devices  15.6 us (23%)
  other arithmetic  3.03 us (5%)
  local copies, waits for them, and re-layouts  2.32 us (3%)
  between operations  0.83 us (1%)
    ppermute x11, starting transfers between devices, swap(): return lax.ppermute(x, axes, pairs)  23.2 us
    ppermute x11, waiting for transfers between devices, swap(): return lax.ppermute(x, axes, pairs)  14.3 us
    pallas_call x4, Pallas kernels, gradients(): pl.pallas_call(functools.partial(grad_kernel, group, first), grid=(count...  9.19 us
    pallas_call x4, Pallas kernels, block_tables(): pl.pallas_call(table_kernel, out_shape=(jax.ShapeDtypeStruct(shape, jnp.f...  6.79 us
    pallas_call x1, Pallas kernels, combine(): pl.pallas_call(combine_kernel, out_shape=jax.ShapeDtypeStruct((2 * tiles...  3.5 us
    sub x1, other arithmetic, adagrad(): return (factors - grad / jnp.sqrt(new_accum), new_accum)  1.59 us
    ppermute x4, waiting for transfers between devices, other(): return lax.ppermute(x, 'rep', [(0, 1), (1, 0)])  1.34 us
  transfers between devices with their start and end apart: 15, of which 9 were waited for; matrix products, arithmetic and copies ran while one was open for 4% of the time, Pallas kernels for 28%

profile of v2, /device:TPU:0, one launch (start us, length us, event | category | flops | bytes accessed | tf_op | source)
XLA Modules:
  0.0 66.5 jit_solution(18192197943056073608)
XLA Ops:
  2.8 4.1 %collective-permute-start.1 = (bf16[1,128,256]{2,1,0:T(8,128)(2,1)S(1)}, bf16[1,128,256]{2,1,0:T(8,128)(2,1)S(1)}, u32[]{:S(2)}, u32[]{:S(2)}) collective-permute-start(bf16[1,128,256]{2,1,0:T(8,128)(2,1)S(1)} %fusion.5), channel_id=1, source_target_pairs={{0,16},{1,9},{2,18},{3,11},{4,20},{5,13},{6,22},{7,15},{8,24},{9,1... | collective-permute-start | bytes 196616 | tf_op jit(solution)/shard_map/ppermute | solution.py:351
  6.9 1.2 %copy-done = f32[1024,256]{1,0:T(8,128)S(1)} copy-done((f32[1024,256]{1,0:T(8,128)S(1)}, f32[1024,256]{1,0:T(8,128)}, u32[]{:S(2)}) %copy-start) | copy-done | bytes 1048600
  9.2 2.3 %collective-permute-start.2 = (bf16[2,128,256]{2,1,0:T(8,128)(2,1)S(1)}, bf16[2,128,256]{2,1,0:T(8,128)(2,1)S(1)}, u32[]{:S(2)}, u32[]{:S(2)}) collective-permute-start(bf16[2,128,256]{2,1,0:T(8,128)(2,1)S(1)} %pad_maximum_fusion.1), channel_id=1, source_target_pairs={{0,8},{1,17},{2,10},{3,19},{4,12},{5,21},{6,14},{7,23},{8,0},{9,25... | collective-permute-start | bytes 393224 | tf_op jit(solution)/shard_map/ppermute | solution.py:351
  11.6 4.0 %collective-permute-done.2 = bf16[2,128,256]{2,1,0:T(8,128)(2,1)S(1)} collective-permute-done((bf16[2,128,256]{2,1,0:T(8,128)(2,1)S(1)}, bf16[2,128,256]{2,1,0:T(8,128)(2,1)S(1)}, u32[]{:S(2)}, u32[]{:S(2)}) %collective-permute-start.2) | collective-permute-done | bytes 131104 | tf_op jit(solution)/shard_map/ppermute | solution.py:351
  15.6 2.2 %collective-permute-start.4 = (bf16[4,128,256]{2,1,0:T(8,128)(2,1)S(1)}, bf16[4,128,256]{2,1,0:T(8,128)(2,1)S(1)}, u32[]{:S(2)}, u32[]{:S(2)}) collective-permute-start(bf16[4,128,256]{2,1,0:T(8,128)(2,1)S(1)} %pad_maximum_fusion.v_ref), channel_id=1, source_target_pairs={{0,2},{1,5},{2,0},{3,7},{4,6},{5,1},{6,4},{7,3},{8,10},{9,13},{10,... | collective-permute-start | bytes 786440 | tf_op jit(solution)/shard_map/ppermute | solution.py:351
  18.1 1.5 %collective-permute-start.6 = (bf16[4,128,256]{2,1,0:T(8,128)(2,1)S(1)}, bf16[4,128,256]{2,1,0:T(8,128)(2,1)S(1)}, u32[]{:S(2)}, u32[]{:S(2)}) collective-permute-start(bf16[4,128,256]{2,1,0:T(8,128)(2,1)S(1)} %pad_maximum_fusion.v_ref), channel_id=1, source_target_pairs={{0,4},{1,3},{2,6},{3,1},{4,0},{5,7},{6,2},{7,5},{8,12},{9,11},{10,... | collective-permute-start | bytes 786440 | tf_op jit(solution)/shard_map/ppermute | solution.py:351
  19.6 4.4 %collective-permute-done.4.v_ref = bf16[4,128,256]{2,1,0:T(8,128)(2,1)S(1)} collective-permute-done((bf16[4,128,256]{2,1,0:T(8,128)(2,1)S(1)}, bf16[4,128,256]{2,1,0:T(8,128)(2,1)S(1)}, u32[]{:S(2)}, u32[]{:S(2)}) %collective-permute-start.4) | collective-permute-done | bytes 262176 | tf_op jit(solution)/shard_map/ppermute | solution.py:351
  24.0 2.4 %collective-permute-start.5 = (bf16[4,128,256]{2,1,0:T(8,128)(2,1)S(1)}, bf16[4,128,256]{2,1,0:T(8,128)(2,1)S(1)}, u32[]{:S(2)}, u32[]{:S(2)}) collective-permute-start(bf16[4,128,256]{2,1,0:T(8,128)(2,1)S(1)} %collective-permute-done.4.v_ref), channel_id=1, source_target_pairs={{0,4},{1,3},{2,6},{3,1},{4,0},{5,7},{6,2},{7,5},{8,12},{9,11},{10,... | collective-permute-start | bytes 786440 | tf_op jit(solution)/shard_map/ppermute | solution.py:351
  26.6 3.5 %combine.1.counts = bf16[257,128,128]{2,1,0:T(8,128)(2,1)S(1)} custom-call(bf16[128,128,128]{2,1,0:T(8,128)(2,1)} %bitcast.21, bf16[128,128,128]{2,1,0:T(8,128)(2,1)} %collective-permute-done.3.par), custom_call_target="tpu_custom_call" | custom-call | tf_op jit(solution)/shard_map/combine/pallas_call | solution.py:120
  30.1 1.6 %tables.7 = (f32[4,1024,128]{2,1,0:T(8,128)S(1)}, bf16[4,1024,128]{2,1,0:T(8,128)(2,1)S(1)}) custom-call(s32[256]{0:T(256)S(1)} %select_reduce_fusion.order, s32[40]{0:T(128)S(1)} %get-tuple-element.51.begin, bf16[257,128,128]{2,1,0:T(8,128)(2,1)S(1)} %combine.1.counts), custom_call_target="tpu_custom_call" | custom-call | tf_op jit(solution)/shard_map/tables/pallas_call | solution.py:179
  31.7 1.8 %tables.6 = (f32[4,1024,128]{2,1,0:T(8,128)S(1)}, bf16[4,1024,128]{2,1,0:T(8,128)(2,1)S(1)}) custom-call(s32[256]{0:T(256)S(1)} %select_reduce_fusion.order, s32[40]{0:T(128)S(1)} %get-tuple-element.52.begin, bf16[257,128,128]{2,1,0:T(8,128)(2,1)S(1)} %combine.1.counts), custom_call_target="tpu_custom_call" | custom-call | tf_op jit(solution)/shard_map/tables/pallas_call | solution.py:179
  33.5 2.3 %gradients.4 = (f32[1024,256]{1,0:T(8,128)S(1)}, bf16[4,256,128]{2,1,0:T(8,128)(2,1)S(1)}) custom-call(f32[32]{0:T(128)S(1)} %get-tuple-element.55.tiles_in, bf16[1024,256]{1,0:T(8,128)(2,1)S(1)} %get-tuple-element.24.u_ref, bf16[256,1024]{1,0:T(8,128)(2,1)S(1)} %get-tuple-element.25.ut_ref, bf16[4,128,256]{2,1,0:T(8,128)(2,1)S(1)} %collective-permute-done.6.v_ref, ...), custom_call_target="tpu_custom_call" | custom-call | tf_op jit(solution)/shard_map/gradients/pallas_call | solution.py:284
  35.9 2.3 %gradients.5 = (f32[1024,256]{1,0:T(8,128)S(1)}, bf16[4,256,128]{2,1,0:T(8,128)(2,1)S(1)}) custom-call(f32[32]{0:T(128)S(1)} %get-tuple-element.56.tiles_in, bf16[1024,256]{1,0:T(8,128)(2,1)S(1)} %get-tuple-element.24.u_ref, bf16[256,1024]{1,0:T(8,128)(2,1)S(1)} %get-tuple-element.25.ut_ref, bf16[4,128,256]{2,1,0:T(8,128)(2,1)S(1)} %collective-permute-done.5.v_ref, ...), custom_call_target="tpu_custom_call" | custom-call | tf_op jit(solution)/shard_map/gradients/pallas_call | solution.py:284
  38.6 1.5 %tables.5 = (f32[4,1024,128]{2,1,0:T(8,128)S(1)}, bf16[4,1024,128]{2,1,0:T(8,128)(2,1)S(1)}) custom-call(s32[256]{0:T(256)S(1)} %select_reduce_fusion.order, s32[40]{0:T(128)S(1)} %get-tuple-element.53.begin, bf16[257,128,128]{2,1,0:T(8,128)(2,1)S(1)} %combine.1.counts), custom_call_target="tpu_custom_call" | custom-call | tf_op jit(solution)/shard_map/tables/pallas_call | solution.py:179
  40.2 1.9 %collective-permute-start.8 = (bf16[4,256,128]{2,1,0:T(8,128)(2,1)S(1)}, bf16[4,256,128]{2,1,0:T(8,128)(2,1)S(1)}, u32[]{:S(2)}, u32[]{:S(2)}) collective-permute-start(bf16[4,256,128]{2,1,0:T(8,128)(2,1)S(1)} %get-tuple-element.39), channel_id=1, source_target_pairs={{0,4},{1,3},{2,6},{3,1},{4,0},{5,7},{6,2},{7,5},{8,12},{9,11},{10,... | collective-permute-start | bytes 786440 | tf_op jit(solution)/shard_map/ppermute | solution.py:351
  42.1 2.3 %gradients.6 = (f32[1024,256]{1,0:T(8,128)S(1)}, f32[4,256,128]{2,1,0:T(8,128)S(1)}) custom-call(f32[32]{0:T(128)S(1)} %get-tuple-element.57.tiles_in, bf16[1024,256]{1,0:T(8,128)(2,1)S(1)} %get-tuple-element.24.u_ref, bf16[256,1024]{1,0:T(8,128)(2,1)S(1)} %get-tuple-element.25.ut_ref, bf16[4,128,256]{2,1,0:T(8,128)(2,1)S(1)} %collective-permute-done.4.v_ref, ...), custom_call_target="tpu_custom_call" | custom-call | tf_op jit(solution)/shard_map/gradients/pallas_call | solution.py:284
  44.7 2.4 %collective-permute-start.10 = (bf16[4,256,128]{2,1,0:T(8,128)(2,1)S(1)}, bf16[4,256,128]{2,1,0:T(8,128)(2,1)S(1)}, u32[]{:S(2)}, u32[]{:S(2)}) collective-permute-start(bf16[4,256,128]{2,1,0:T(8,128)(2,1)S(1)} %add_convert_fusion), channel_id=1, source_target_pairs={{0,2},{1,5},{2,0},{3,7},{4,6},{5,1},{6,4},{7,3},{8,10},{9,13},{10,... | collective-permute-start | bytes 786440 | tf_op jit(solution)/shard_map/ppermute | solution.py:351
  47.1 1.9 %tables.4 = (f32[4,1024,128]{2,1,0:T(8,128)S(1)}, bf16[4,1024,128]{2,1,0:T(8,128)(2,1)S(1)}) custom-call(s32[256]{0:T(256)S(1)} %select_reduce_fusion.order, s32[40]{0:T(128)S(1)} %get-tuple-element.54.begin, bf16[257,128,128]{2,1,0:T(8,128)(2,1)S(1)} %combine.1.counts), custom_call_target="tpu_custom_call" | custom-call | tf_op jit(solution)/shard_map/tables/pallas_call | solution.py:179
  48.9 2.3 %gradients.7 = (f32[1024,256]{1,0:T(8,128)S(1)}, f32[4,256,128]{2,1,0:T(8,128)S(1)}) custom-call(f32[32]{0:T(128)S(1)} %get-tuple-element.58.tiles_in, bf16[1024,256]{1,0:T(8,128)(2,1)S(1)} %get-tuple-element.24.u_ref, bf16[256,1024]{1,0:T(8,128)(2,1)S(1)} %get-tuple-element.25.ut_ref, bf16[4,128,256]{2,1,0:T(8,128)(2,1)S(1)} %pad_maximum_fusion.v_ref, ...), custom_call_target="tpu_custom_call" | custom-call | tf_op jit(solution)/shard_map/gradients/pallas_call | solution.py:284
  51.5 5.2 %collective-permute-start.11 = (bf16[256,128]{1,0:T(8,128)(2,1)S(1)}, bf16[256,128]{1,0:T(8,128)(2,1)S(1)}, u32[]{:S(2)}, u32[]{:S(2)}) collective-permute-start(bf16[256,128]{1,0:T(8,128)(2,1)S(1)} %get-tuple-element.48), channel_id=1, source_target_pairs={{0,24},{1,25},{2,26},{3,27},{4,28},{5,29},{6,30},{7,31},{8,16},{9,... | collective-permute-start | bytes 196616 | tf_op jit(solution)/shard_map/ppermute | solution.py:351
  57.4 2.4 %collective-permute-done.11 = bf16[256,128]{1,0:T(8,128)(2,1)S(1)} collective-permute-done((bf16[256,128]{1,0:T(8,128)(2,1)S(1)}, bf16[256,128]{1,0:T(8,128)(2,1)S(1)}, u32[]{:S(2)}, u32[]{:S(2)}) %collective-permute-start.11) | collective-permute-done | bytes 65568 | tf_op jit(solution)/shard_map/ppermute | solution.py:351
  59.8 1.8 %collective-permute-done.12 = bf16[256,128]{1,0:T(8,128)(2,1)S(1)} collective-permute-done((bf16[256,128]{1,0:T(8,128)(2,1)S(1)}, bf16[256,128]{1,0:T(8,128)(2,1)S(1)}, u32[]{:S(2)}, u32[]{:S(2)}) %collective-permute-start.12) | collective-permute-done | bytes 65568 | tf_op jit(solution)/shard_map/ppermute | solution.py:351
  62.6 1.3 %collective-permute-done.14.there = f32[256,128]{1,0:T(8,128)S(1)} collective-permute-done((f32[256,128]{1,0:T(8,128)S(1)}, f32[256,128]{1,0:T(8,128)S(1)}, u32[]{:S(2)}, u32[]{:S(2)}) %collective-permute-start.14) | collective-permute-done | bytes 131104 | tf_op jit(solution)/shard_map/ppermute | solution.py:354
  64.9 1.6 %multiply_subtract_fusion = (f32[1024,256]{1,0:T(8,128)}, f32[1024,256]{1,0:T(8,128)}) fusion(f32[1024,256]{1,0:T(8,128)S(1)} %copy-done.1, f32[1024,256]{1,0:T(8,128)S(1)} %copy-done.4, f32[1024,256]{1,0:T(8,128)S(1)} %get-tuple-element.37, f32[1024,256]{1,0:T(8,128)S(1)} %collective-permute-done.7), kind=kLoop, calls=%fused_computation | loop fusion | flops 1310720 | bytes 6291456 | tf_op jit(solution)/shard_map/sub | solution.py:66
  (43 shorter events, 7.4 us)
Async XLA Ops:
  0.6 26.0 %collective-permute-start.3 = (bf16[128,128,128]{2,1,0:T(8,128)(2,1)}, bf16[128,128,128]{2,1,0:T(8,128)(2,1)}, u32[]{:S(2)}, u32[]{:S(2)}) collective-permute-start(bf16[128,128,128]{2,1,0:T(8,128)(2,1)} %bitcast.20), channel_id=1, source_target_pairs={{0,1},{1,0},{2,3},{3,2},{4,5},{5,4},{6,7},{7,6},{8,9},{9,8},{10,11... | collective-permute-start | bytes 12582920 | tf_op jit(solution)/shard_map/ppermute | solution.py:354
  1.9 6.6 %collective-permute-start = (s32[128]{0:T(128)S(1)}, s32[128]{0:T(128)S(1)}, u32[]{:S(2)}, u32[]{:S(2)}) collective-permute-start(s32[128]{0:T(128)S(1)} %add_bitcast_fusion), channel_id=1, source_target_pairs={{0,1},{1,0},{2,3},{3,2},{4,5},{5,4},{6,7},{7,6},{8,9},{9,8},{10,11... | collective-permute-start | bytes 1544 | tf_op jit(solution)/shard_map/ppermute | solution.py:354
  2.8 6.4 %collective-permute-start.1 = (bf16[1,128,256]{2,1,0:T(8,128)(2,1)S(1)}, bf16[1,128,256]{2,1,0:T(8,128)(2,1)S(1)}, u32[]{:S(2)}, u32[]{:S(2)}) collective-permute-start(bf16[1,128,256]{2,1,0:T(8,128)(2,1)S(1)} %fusion.5), channel_id=1, source_target_pairs={{0,16},{1,9},{2,18},{3,11},{4,20},{5,13},{6,22},{7,15},{8,24},{9,1... | collective-permute-start | bytes 196616 | tf_op jit(solution)/shard_map/ppermute | solution.py:351
  6.9 1.2 %copy-start = (f32[1024,256]{1,0:T(8,128)S(1)}, f32[1024,256]{1,0:T(8,128)}, u32[]{:S(2)}) copy-start(f32[1024,256]{1,0:T(8,128)} %f_ref.2) | copy-start | bytes 3145732
  9.2 6.4 %collective-permute-start.2 = (bf16[2,128,256]{2,1,0:T(8,128)(2,1)S(1)}, bf16[2,128,256]{2,1,0:T(8,128)(2,1)S(1)}, u32[]{:S(2)}, u32[]{:S(2)}) collective-permute-start(bf16[2,128,256]{2,1,0:T(8,128)(2,1)S(1)} %pad_maximum_fusion.1), channel_id=1, source_target_pairs={{0,8},{1,17},{2,10},{3,19},{4,12},{5,21},{6,14},{7,23},{8,0},{9,25... | collective-permute-start | bytes 393224 | tf_op jit(solution)/shard_map/ppermute | solution.py:351
  15.6 8.4 %collective-permute-start.4 = (bf16[4,128,256]{2,1,0:T(8,128)(2,1)S(1)}, bf16[4,128,256]{2,1,0:T(8,128)(2,1)S(1)}, u32[]{:S(2)}, u32[]{:S(2)}) collective-permute-start(bf16[4,128,256]{2,1,0:T(8,128)(2,1)S(1)} %pad_maximum_fusion.v_ref), channel_id=1, source_target_pairs={{0,2},{1,5},{2,0},{3,7},{4,6},{5,1},{6,4},{7,3},{8,10},{9,13},{10,... | collective-permute-start | bytes 786440 | tf_op jit(solution)/shard_map/ppermute | solution.py:351
  18.1 15.5 %collective-permute-start.6 = (bf16[4,128,256]{2,1,0:T(8,128)(2,1)S(1)}, bf16[4,128,256]{2,1,0:T(8,128)(2,1)S(1)}, u32[]{:S(2)}, u32[]{:S(2)}) collective-permute-start(bf16[4,128,256]{2,1,0:T(8,128)(2,1)S(1)} %pad_maximum_fusion.v_ref), channel_id=1, source_target_pairs={{0,4},{1,3},{2,6},{3,1},{4,0},{5,7},{6,2},{7,5},{8,12},{9,11},{10,... | collective-permute-start | bytes 786440 | tf_op jit(solution)/shard_map/ppermute | solution.py:351
  24.0 11.8 %collective-permute-start.5 = (bf16[4,128,256]{2,1,0:T(8,128)(2,1)S(1)}, bf16[4,128,256]{2,1,0:T(8,128)(2,1)S(1)}, u32[]{:S(2)}, u32[]{:S(2)}) collective-permute-start(bf16[4,128,256]{2,1,0:T(8,128)(2,1)S(1)} %collective-permute-done.4.v_ref), channel_id=1, source_target_pairs={{0,4},{1,3},{2,6},{3,1},{4,0},{5,7},{6,2},{7,5},{8,12},{9,11},{10,... | collective-permute-start | bytes 786440 | tf_op jit(solution)/shard_map/ppermute | solution.py:351
  38.2 6.4 %collective-permute-start.9 = (bf16[4,256,128]{2,1,0:T(8,128)(2,1)S(1)}, bf16[4,256,128]{2,1,0:T(8,128)(2,1)S(1)}, u32[]{:S(2)}, u32[]{:S(2)}) collective-permute-start(bf16[4,256,128]{2,1,0:T(8,128)(2,1)S(1)} %get-tuple-element.41), channel_id=1, source_target_pairs={{0,4},{1,3},{2,6},{3,1},{4,0},{5,7},{6,2},{7,5},{8,12},{9,11},{10,... | collective-permute-start | bytes 786440 | tf_op jit(solution)/shard_map/ppermute | solution.py:351
  40.2 11.2 %collective-permute-start.8 = (bf16[4,256,128]{2,1,0:T(8,128)(2,1)S(1)}, bf16[4,256,128]{2,1,0:T(8,128)(2,1)S(1)}, u32[]{:S(2)}, u32[]{:S(2)}) collective-permute-start(bf16[4,256,128]{2,1,0:T(8,128)(2,1)S(1)} %get-tuple-element.39), channel_id=1, source_target_pairs={{0,4},{1,3},{2,6},{3,1},{4,0},{5,7},{6,2},{7,5},{8,12},{9,11},{10,... | collective-permute-start | bytes 786440 | tf_op jit(solution)/shard_map/ppermute | solution.py:351
  44.7 6.7 %collective-permute-start.10 = (bf16[4,256,128]{2,1,0:T(8,128)(2,1)S(1)}, bf16[4,256,128]{2,1,0:T(8,128)(2,1)S(1)}, u32[]{:S(2)}, u32[]{:S(2)}) collective-permute-start(bf16[4,256,128]{2,1,0:T(8,128)(2,1)S(1)} %add_convert_fusion), channel_id=1, source_target_pairs={{0,2},{1,5},{2,0},{3,7},{4,6},{5,1},{6,4},{7,3},{8,10},{9,13},{10,... | collective-permute-start | bytes 786440 | tf_op jit(solution)/shard_map/ppermute | solution.py:351
  51.2 12.7 %copy-start.2 = (f32[256,256]{1,0:T(8,128)S(1)}, f32[256,256]{1,0:T(8,128)}, u32[]{:S(2)}) copy-start(f32[256,256]{1,0:T(8,128)} %f_ref.3) | copy-start | bytes 786436
  51.2 12.7 %copy-start.3 = (f32[256,256]{1,0:T(8,128)S(1)}, f32[256,256]{1,0:T(8,128)}, u32[]{:S(2)}) copy-start(f32[256,256]{1,0:T(8,128)} %a_ref.1) | copy-start | bytes 786436
  51.2 13.7 %copy-start.1 = (f32[1024,256]{1,0:T(8,128)S(1)}, f32[1024,256]{1,0:T(8,128)}, u32[]{:S(2)}) copy-start(f32[1024,256]{1,0:T(8,128)} %f_ref.2) | copy-start | bytes 3145732
  51.3 13.7 %copy-start.4 = (f32[1024,256]{1,0:T(8,128)S(1)}, f32[1024,256]{1,0:T(8,128)}, u32[]{:S(2)}) copy-start(f32[1024,256]{1,0:T(8,128)} %param.9) | copy-start | bytes 3145732
  51.3 13.7 %collective-permute-start.7 = (f32[1024,256]{1,0:T(8,128)S(1)}, f32[1024,256]{1,0:T(8,128)S(1)}, u32[]{:S(2)}, u32[]{:S(2)}) collective-permute-start(f32[1024,256]{1,0:T(8,128)S(1)} %get-tuple-element.37), channel_id=1, source_target_pairs={{0,1},{1,0},{2,3},{3,2},{4,5},{5,4},{6,7},{7,6},{8,9},{9,8},{10,11... | collective-permute-start | bytes 3145736 | tf_op jit(solution)/shard_map/ppermute | solution.py:354
  51.5 8.2 %collective-permute-start.11 = (bf16[256,128]{1,0:T(8,128)(2,1)S(1)}, bf16[256,128]{1,0:T(8,128)(2,1)S(1)}, u32[]{:S(2)}, u32[]{:S(2)}) collective-permute-start(bf16[256,128]{1,0:T(8,128)(2,1)S(1)} %get-tuple-element.48), channel_id=1, source_target_pairs={{0,24},{1,25},{2,26},{3,27},{4,28},{5,29},{6,30},{7,31},{8,16},{9,... | collective-permute-start | bytes 196616 | tf_op jit(solution)/shard_map/ppermute | solution.py:351
  56.7 4.8 %collective-permute-start.12 = (bf16[256,128]{1,0:T(8,128)(2,1)S(1)}, bf16[256,128]{1,0:T(8,128)(2,1)S(1)}, u32[]{:S(2)}, u32[]{:S(2)}) collective-permute-start(bf16[256,128]{1,0:T(8,128)(2,1)S(1)} %get-tuple-element.50), channel_id=1, source_target_pairs={{0,8},{1,17},{2,10},{3,19},{4,12},{5,21},{6,14},{7,23},{8,0},{9,25... | collective-permute-start | bytes 196616 | tf_op jit(solution)/shard_map/ppermute | solution.py:351
  56.7 5.7 %collective-permute-start.13 = (bf16[256,128]{1,0:T(8,128)(2,1)S(1)}, bf16[256,128]{1,0:T(8,128)(2,1)S(1)}, u32[]{:S(2)}, u32[]{:S(2)}) collective-permute-start(bf16[256,128]{1,0:T(8,128)(2,1)S(1)} %get-tuple-element.49), channel_id=1, source_target_pairs={{0,16},{1,9},{2,18},{3,11},{4,20},{5,13},{6,22},{7,15},{8,24},{9,1... | collective-permute-start | bytes 196616 | tf_op jit(solution)/shard_map/ppermute | solution.py:351
  62.5 1.4 %collective-permute-start.14 = (f32[256,128]{1,0:T(8,128)S(1)}, f32[256,128]{1,0:T(8,128)S(1)}, u32[]{:S(2)}, u32[]{:S(2)}) collective-permute-start(f32[256,128]{1,0:T(8,128)S(1)} %fusion.4.here), channel_id=1, source_target_pairs={{0,1},{1,0},{2,3},{3,2},{4,5},{5,4},{6,7},{7,6},{8,9},{9,8},{10,11... | collective-permute-start | bytes 393224 | tf_op jit(solution)/shard_map/ppermute | solution.py:354
